TPU v7x, 32 devices: a whole 2x2x4 slice. The times are simulated.
32 devices in a mesh: dp: 8 (over z, x), tensor: 4 (over y, core).
Axes of the slice: x: 2, y: 2, z: 4, core: 2. Of those that a mesh axis runs over, the one named last changes fastest.
Arguments:
- tokens: bfloat16 [16384, 768], P('dp'), may hold values from -6 to 6
- seq_lengths: int32 [8, 9], P('dp'), may hold values from 1 to 512, 2048 in all within a row
- query_weight: bfloat16 [768, 768], P(None, 'tensor'), may hold values from -0.21875 to 0.21875
- key_weight: bfloat16 [768, 768], P(None, 'tensor'), may hold values from -0.21875 to 0.21875
- value_weight: bfloat16 [768, 768], P(None, 'tensor'), may hold values from -0.21875 to 0.21875
- out_weight: bfloat16 [768, 768], P('tensor'), may hold values from -0.875 to 0.875
- ffn_in: bfloat16 [768, 3072], P(None, 'tensor'), may hold values from -0.21875 to 0.21875
- ffn_out: bfloat16 [3072, 768], P('tensor'), may hold values from -0.109375 to 0.109375
- gain_attn: float32 [768], replicated, may hold values from 0.5 to 1.5
- gain_ffn: float32 [768], replicated, may hold values from 0.5 to 1.5
- query_down: bfloat16 [768, 8], replicated, may hold values from -0.21875 to 0.21875
- value_down: bfloat16 [768, 8], replicated, may hold values from -0.21875 to 0.21875
- query_up: bfloat16 [8, 12, 64], P(None, 'tensor'), may hold values from -1.078125 to 1.078125
- value_up: bfloat16 [8, 12, 64], P(None, 'tensor'), may hold values from -1.078125 to 1.078125
- cotangent: bfloat16 [16384, 768], P('dp'), may hold values from -6 to 6
Outputs:
- activations: bfloat16 [16384, 768], P(('dp', 'tensor'))
- input_grad: float32 [16384, 768], P(('dp', 'tensor'))
- query_up_grad: float32 [8, 12, 64], P(None, 'tensor', 'dp')
- value_up_grad: float32 [8, 12, 64], P(None, 'tensor', 'dp')
Inputs may be any that keep to these rules, and one draw needn't show every extreme that they name: `seq_lengths`: row b holds the lengths of the 8 sequences packed from the start of the b-th block of 2048 slots, in order, then the number of padding slots at the block's end; every row sums to 2048 and reaches 512.
All inputs are finite; a program needn't handle non-finite values.
Results may differ from a plain program's by a relative error of at most 0.025.
Values may be sent and summed in bfloat16 or wider, within the bound.
A program may use at most 128 MiB of HBM per device.

v0:
```python
import jax
import jax.numpy as jnp
from jax import lax
from jax.sharding import PartitionSpec as P

H = 12
HD = 64
R = 8
SEQ = 512


EPSILON = 1e-05
NEGATIVE = -1e30


def normalize(vector, scale_gain):
    average = jnp.mean(vector, axis=-1, keepdims=True)
    centered = vector - average
    inverse = lax.rsqrt(jnp.mean(centered * centered, axis=-1, keepdims=True) + EPSILON)
    unit_rows = centered * inverse
    return (unit_rows * scale_gain, unit_rows, inverse)


def normalize_back(upstream, unit_rows, inverse, scale_gain):
    scaled = upstream * scale_gain
    return inverse * (
        scaled
        - jnp.mean(scaled, axis=-1, keepdims=True)
        - unit_rows * jnp.mean(scaled * unit_rows, axis=-1, keepdims=True)
    )


def segment_ids(seg_ends, positions, block_rows):
    counted = jnp.sum((positions[:, None] >= seg_ends[None, :]).astype(jnp.int32), axis=1)
    inside = (positions >= 0) & (positions < block_rows)
    segment = jnp.where(inside, counted, -2)
    is_valid = inside & (counted < seg_ends.shape[0] - 1)
    return (segment, is_valid)


def transpose_dot(left_side, right_side):
    return lax.dot_general(
        left_side, right_side, (((1,), (1,)), ((), ())), preferred_element_type=jnp.float32
    )


def block_scores(
    block_index,
    queries,
    keys_ext,
    values_ext,
    seg_query,
    seg_keys,
    valid_query,
    head_count,
    block_span,
):
    col_width = queries.shape[1]
    head_size = col_width // head_count
    row_start = block_index * block_span
    query_block = lax.dynamic_slice_in_dim(queries, row_start, block_span, 0).reshape(
        block_span, head_count, head_size
    )
    key_block = lax.dynamic_slice_in_dim(keys_ext, row_start, 3 * block_span, 0).reshape(
        3 * block_span, head_count, head_size
    )
    value_block = lax.dynamic_slice_in_dim(values_ext, row_start, 3 * block_span, 0).reshape(
        3 * block_span, head_count, head_size
    )
    seg_rows = lax.dynamic_slice_in_dim(seg_query, row_start, block_span, 0)
    seg_cols = lax.dynamic_slice_in_dim(seg_keys, row_start, 3 * block_span, 0)
    valid_rows = lax.dynamic_slice_in_dim(valid_query, row_start, block_span, 0)
    allowed = (seg_rows[:, None] == seg_cols[None, :]) & valid_rows[:, None]
    scores = jnp.einsum(
        "qhd,khd->hqk", query_block, key_block, preferred_element_type=jnp.float32
    ) * head_size ** (-0.5)
    masked = jnp.where(allowed[None], scores, NEGATIVE)
    return (query_block, key_block, value_block, allowed, masked, valid_rows)


def attend_forward(
    block_index,
    queries,
    keys_ext,
    values_ext,
    seg_query,
    seg_keys,
    valid_query,
    head_count,
    block_span,
):
    query_block, key_block, value_block, allowed, masked, valid_rows = block_scores(
        block_index,
        queries,
        keys_ext,
        values_ext,
        seg_query,
        seg_keys,
        valid_query,
        head_count,
        block_span,
    )
    row_max = jnp.max(masked, axis=-1, keepdims=True)
    weights = jnp.where(allowed[None], jnp.exp(masked - row_max), 0.0)
    row_total = (
        jnp.sum(weights, axis=-1, keepdims=True)
        + (1.0 - valid_rows.astype(jnp.float32))[None, :, None]
    )
    probability = (weights / row_total).astype(jnp.bfloat16)
    mixed_rows = jnp.einsum(
        "hqk,khd->qhd", probability, value_block, preferred_element_type=jnp.float32
    )
    return (
        mixed_rows.reshape(block_span, queries.shape[1]),
        (row_max + jnp.log(row_total))[:, :, 0],
    )


def attend_backward(
    block_index,
    queries,
    keys_ext,
    values_ext,
    seg_query,
    seg_keys,
    valid_query,
    head_count,
    block_span,
    log_total,
    grad_context,
):
    query_block, key_block, value_block, allowed, masked, valid_rows = block_scores(
        block_index,
        queries,
        keys_ext,
        values_ext,
        seg_query,
        seg_keys,
        valid_query,
        head_count,
        block_span,
    )
    col_width = queries.shape[1]
    head_size = col_width // head_count
    score_scale = head_size ** (-0.5)
    stored = log_total[block_index]
    probability = jnp.where(allowed[None], jnp.exp(masked - stored[:, :, None]), 0.0)
    grad_block = lax.dynamic_slice_in_dim(
        grad_context, block_index * block_span, block_span, 0
    ).reshape(block_span, head_count, head_size)
    grad_prob = jnp.einsum(
        "qhd,khd->hqk", grad_block, value_block, preferred_element_type=jnp.float32
    )
    row_delta = jnp.sum(probability * grad_prob, axis=-1, keepdims=True)
    grad_scores = (probability * (grad_prob - row_delta)).astype(jnp.bfloat16)
    grad_query = (
        jnp.einsum("hqk,khd->qhd", grad_scores, key_block, preferred_element_type=jnp.float32)
        * score_scale
    )
    grad_key = (
        jnp.einsum("hqk,qhd->khd", grad_scores, query_block, preferred_element_type=jnp.float32)
        * score_scale
    )
    grad_value = jnp.einsum(
        "hqk,qhd->khd",
        probability.astype(jnp.bfloat16),
        grad_block,
        preferred_element_type=jnp.float32,
    )
    return (
        grad_query.reshape(block_span, col_width),
        grad_key.reshape(3 * block_span, col_width),
        grad_value.reshape(3 * block_span, col_width),
    )


def on_device(
    tokens,
    seq_lengths,
    query_weight,
    key_weight,
    value_weight,
    out_weight,
    ffn_in,
    ffn_out,
    gain_attn,
    gain_ffn,
    query_down,
    value_down,
    query_up,
    value_up,
    cotangent,
):
    groups = lax.axis_size("tensor")
    member = lax.axis_index("tensor")
    block_span = SEQ
    block_rows = tokens.shape[0]
    own_rows = block_rows // groups
    seg_ends = jnp.cumsum(seq_lengths[0])
    w_query, w_key, w_value, w_inner, w_out, w_ffn_out, up_query, up_value = (
        query_weight,
        key_weight,
        value_weight,
        ffn_in,
        out_weight,
        ffn_out,
        query_up,
        value_up,
    )
    first_row = 0
    head_count = H // groups
    row_count = tokens.shape[0]
    col_width = w_query.shape[1]
    up_query_flat = up_query.reshape(R, col_width)
    up_value_flat = up_value.reshape(R, col_width)
    down_query_wide = query_down.astype(jnp.float32)
    down_value_wide = value_down.astype(jnp.float32)
    low_query = jnp.dot(tokens, query_down, preferred_element_type=jnp.float32).astype(jnp.bfloat16)
    low_value = jnp.dot(tokens, value_down, preferred_element_type=jnp.float32).astype(jnp.bfloat16)
    queries = (
        jnp.dot(tokens, w_query, preferred_element_type=jnp.float32)
        + 2.0 * jnp.dot(low_query, up_query_flat, preferred_element_type=jnp.float32)
    ).astype(jnp.bfloat16)
    key_rows = jnp.dot(tokens, w_key, preferred_element_type=jnp.float32).astype(jnp.bfloat16)
    values = (
        jnp.dot(tokens, w_value, preferred_element_type=jnp.float32)
        + 2.0 * jnp.dot(low_value, up_value_flat, preferred_element_type=jnp.float32)
    ).astype(jnp.bfloat16)
    key_value = jnp.stack([key_rows, values])
    key_value_ext = jnp.pad(key_value, ((0, 0), (block_span, block_span), (0, 0)))
    keys_ext = key_value_ext[0]
    values_ext = key_value_ext[1]
    positions = first_row - block_span + jnp.arange(row_count + 2 * block_span, dtype=jnp.int32)
    seg_keys, valid_keys = segment_ids(seg_ends, positions, block_rows)
    seg_query = seg_keys[block_span : block_span + row_count]
    valid_query = valid_keys[block_span : block_span + row_count]
    valid_rows = valid_query.astype(jnp.float32)[:, None]
    block_count = row_count // block_span

    def forward_block(block_index):
        return attend_forward(
            block_index,
            queries,
            keys_ext,
            values_ext,
            seg_query,
            seg_keys,
            valid_query,
            head_count,
            block_span,
        )

    context_blocks, log_total = lax.map(forward_block, jnp.arange(block_count))
    context = context_blocks.reshape(row_count, col_width).astype(jnp.bfloat16)
    attn_out = lax.psum(
        jnp.dot(context, w_out, preferred_element_type=jnp.float32).astype(jnp.bfloat16), "tensor"
    ).astype(jnp.float32)
    normed, unit_one, inverse_one = normalize(tokens.astype(jnp.float32) + attn_out, gain_attn)
    normed_low = normed.astype(jnp.bfloat16)
    pre_act = jnp.dot(normed_low, w_inner, preferred_element_type=jnp.float32)
    active = jax.nn.gelu(pre_act, approximate=False).astype(jnp.bfloat16)
    ffn_result = lax.psum(
        jnp.dot(active, w_ffn_out, preferred_element_type=jnp.float32).astype(jnp.bfloat16),
        "tensor",
    ).astype(jnp.float32)
    final_rows, unit_two, inverse_two = normalize(normed + ffn_result, gain_ffn)
    final_rows = final_rows * valid_rows
    grad_final = cotangent.astype(jnp.float32) * valid_rows
    grad_mid = normalize_back(grad_final, unit_two, inverse_two, gain_ffn)
    grad_active = transpose_dot(grad_mid.astype(jnp.bfloat16), w_ffn_out)
    recomputed = jnp.dot(
        lax.optimization_barrier(normed_low), w_inner, preferred_element_type=jnp.float32
    )
    gelu_pull = jax.vjp(lambda argument: jax.nn.gelu(argument, approximate=False), recomputed)[1]
    grad_pre = gelu_pull(grad_active)[0].astype(jnp.bfloat16)
    grad_normed = grad_mid + lax.psum(
        transpose_dot(grad_pre, w_inner).astype(jnp.bfloat16), "tensor"
    ).astype(jnp.float32)
    grad_mixed = normalize_back(grad_normed, unit_one, inverse_one, gain_attn)
    grad_context = transpose_dot(grad_mixed.astype(jnp.bfloat16), w_out).astype(jnp.bfloat16)

    def back_step(accumulated, block_index):
        key_total, value_total = accumulated
        grad_query, grad_key, grad_value = attend_backward(
            block_index,
            queries,
            keys_ext,
            values_ext,
            seg_query,
            seg_keys,
            valid_query,
            head_count,
            block_span,
            log_total,
            grad_context,
        )
        row_start = block_index * block_span
        key_total = lax.dynamic_update_slice_in_dim(
            key_total,
            lax.dynamic_slice_in_dim(key_total, row_start, 3 * block_span, 0) + grad_key,
            row_start,
            0,
        )
        value_total = lax.dynamic_update_slice_in_dim(
            value_total,
            lax.dynamic_slice_in_dim(value_total, row_start, 3 * block_span, 0) + grad_value,
            row_start,
            0,
        )
        return ((key_total, value_total), grad_query)

    empty_ext = jnp.zeros((row_count + 2 * block_span, col_width), jnp.float32)
    (key_total, value_total), query_grads = lax.scan(
        back_step, (empty_ext, empty_ext), jnp.arange(block_count)
    )
    key_middle = key_total[block_span : block_span + row_count]
    value_middle = value_total[block_span : block_span + row_count]
    grad_queries = query_grads.reshape(row_count, col_width).astype(jnp.bfloat16)
    grad_keys = key_middle.astype(jnp.bfloat16)
    grad_values = value_middle.astype(jnp.bfloat16)
    input_term = (
        transpose_dot(grad_queries, w_query)
        + transpose_dot(grad_keys, w_key)
        + transpose_dot(grad_values, w_value)
    )
    low_query_grad = 2.0 * transpose_dot(grad_queries, up_query_flat)
    low_value_grad = 2.0 * transpose_dot(grad_values, up_value_flat)
    input_term = input_term + jnp.dot(
        low_query_grad,
        down_query_wide.T,
        precision=lax.Precision.HIGHEST,
        preferred_element_type=jnp.float32,
    )
    input_term = input_term + jnp.dot(
        low_value_grad,
        down_value_wide.T,
        precision=lax.Precision.HIGHEST,
        preferred_element_type=jnp.float32,
    )
    grad_input = grad_mixed + lax.psum(input_term.astype(jnp.bfloat16), "tensor").astype(
        jnp.float32
    )
    adapter_query = (
        2.0
        * lax.dot_general(
            low_query, grad_queries, (((0,), (0,)), ((), ())), preferred_element_type=jnp.float32
        )
    ).reshape(R, head_count, HD)
    adapter_value = (
        2.0
        * lax.dot_general(
            low_value, grad_values, (((0,), (0,)), ((), ())), preferred_element_type=jnp.float32
        )
    ).reshape(R, head_count, HD)
    grad_up_query, grad_up_value = (
        lax.psum_scatter(adapter_query, "dp", scatter_dimension=2, tiled=True),
        lax.psum_scatter(adapter_value, "dp", scatter_dimension=2, tiled=True),
    )
    out_rows = lax.dynamic_slice_in_dim(final_rows, member * own_rows, own_rows, 0).astype(
        jnp.bfloat16
    )
    out_grads = lax.dynamic_slice_in_dim(grad_input, member * own_rows, own_rows, 0)
    return (out_rows, out_grads, grad_up_query, grad_up_value)


def solution(mesh):
    in_specs = (
        P("dp", None),
        P("dp", None),
        P(None, "tensor"),
        P(None, "tensor"),
        P(None, "tensor"),
        P("tensor", None),
        P(None, "tensor"),
        P("tensor", None),
        P(),
        P(),
        P(),
        P(),
        P(None, "tensor", None),
        P(None, "tensor", None),
        P("dp", None),
    )
    out_specs = (
        P(("dp", "tensor"), None),
        P(("dp", "tensor"), None),
        P(None, "tensor", "dp"),
        P(None, "tensor", "dp"),
    )
    return jax.shard_map(
        on_device, mesh=mesh, in_specs=in_specs, out_specs=out_specs, check_vma=False
    )
```

profile of v0, /device:TPU:0, one launch (start us, length us, event | category | flops | bytes accessed | tf_op | source)
XLA Modules:
  0.0 639.0 jit_solution(7620324804941043654)
XLA Ops:
  23.7 58.6 %while.26 = (s32[]{:T(128)}, bf16[4,512,192]{1,2,0:T(8,128)(2,1)}, f32[4,3,512]{2,1,0:T(4,128)}, s32[4]{0:T(128)S(1)}, bf16[3072,192]{0,1:T(8,128)(2,1)S(1)}, /*...) while((s32[]{:T(128)}, bf16[4,512,192]{1,2,0:T(8,128)(2,1)}, ...), condition=%wide.region_5.6_spmd, body=%wide.region_2.5_spmd.sunk | while | flops 638585344 | bytes 36271876 | solution.py:253
  88.1 71.0 %all-reduce.9.cloned.1.call-done = bf16[2048,768]{1,0:T(8,128)(2,1)} async-done(((bf16[2048,768]{1,0:T(8,128)(2,1)}), bf16[2048,768]{1,0:T(8,128)(2,1)}) %all-reduce.9.cloned.1.call-update) | async-done | bytes 3145744 | tf_op jit(solution)/shard_map/psum | solution.py:255
  168.0 19.9 %convolution_convert_fusion.1 = bf16[2048,768]{1,0:T(8,128)(2,1)} fusion(bf16[768,768]{1,0:T(8,128)(2,1)S(1)} %copy-done.48, bf16[2048,768]{1,0:T(8,128)(2,1)} %multiply_convert_fusion.1, bf16[768,768]{1,0:T(8,128)(2,1)S(1)} %copy-done), kind=kOutput, calls=%fused_computation.101 | convolution fusion | flops 4935647232 | bytes 8650752 | tf_op jit(solution)/shard_map/dot_general | solution.py:263
  188.4 7.1 %fusion.131 = f32[2048,768]{1,0:T(8,128)} fusion(bf16[2048,768]{1,0:T(8,128)(2,1)} %multiply_convert_fusion.1, bf16[768,768]{1,0:T(8,128)(2,1)S(1)} %copy-done), kind=kOutput, calls=%fused_computation.218 | convolution fusion | flops 2415919104 | bytes 10616832 | tf_op jit(solution)/shard_map/dot_general | solution.py:271
  195.5 61.1 %all-reduce.11.cloned.1.call-done = bf16[2048,768]{1,0:T(8,128)(2,1)} async-done(((bf16[2048,768]{1,0:T(8,128)(2,1)}), bf16[2048,768]{1,0:T(8,128)(2,1)}) %all-reduce.11.cloned.1.call-update) | async-done | bytes 3145744 | tf_op jit(solution)/shard_map/psum | solution.py:262
  256.6 5.9 fusion.58
  277.4 22.6 %convolution_convert_fusion = bf16[2048,768]{1,0:T(8,128)(2,1)} fusion(bf16[768,768]{1,0:T(8,128)(2,1)S(1)} %copy-done, f32[2048,768]{1,0:T(8,128)} %fusion.131, bf16[768,768]{1,0:T(8,128)(2,1)S(1)} %copy-done.48, f32[2048,768]{1,0:T(8,128)} %subtract_multiply_fusion.1), kind=kOutput, calls=%fused_computation.100 | convolution fusion | flops 4948230144 | bytes 18087936 | tf_op jit(solution)/shard_map/dot_general | solution.py:42
  300.0 68.6 %all-reduce.13.cloned.1.call-done = bf16[2048,768]{1,0:T(8,128)(2,1)} async-done(((bf16[2048,768]{1,0:T(8,128)(2,1)}), bf16[2048,768]{1,0:T(8,128)(2,1)}) %all-reduce.13.cloned.1.call-update) | async-done | bytes 3145744 | tf_op jit(solution)/shard_map/psum | solution.py:276
  368.7 8.4 %fusion.59 = (f32[2048]{0:T(1024)S(1)}, f32[2048]{0:T(1024)S(1)}) fusion(f32[768]{0:T(1024)S(1)} %copy-done.38, f32[2048,768]{1,0:T(8,128)} %subtract_multiply_fusion.1, bf16[2048,768]{1,0:T(8,128)(2,1)} %all-reduce.13.cloned.1.call-done, f32[2048]{0:T(1024)S(1)} %add_rsqrt_fusion.1, f32[2048]{0:T(1024)S(1)} %copy-done.33, ...), kind=kLoop, calls=%fused_computation.123 | loop fusion | flops 17297408 | bytes 15764480 | tf_op jit(solution)/shard_map/reduce_sum | solution.py:28
  377.1 5.2 subtract_multiply_fusion
  388.6 154.5 %while.27 = (s32[]{:T(128)}, f32[3072,192]{0,1:T(8,128)}, f32[3072,192]{0,1:T(8,128)S(1)}, bf16[4,512,192]{1,2,0:T(8,128)(2,1)}, s32[4]{0:T(128)}, /*index=5*/bf...) while((s32[]{:T(128)}, f32[3072,192]{0,1:T(8,128)}, ...), condition=%wide.region_19.20_spmd, body=%wide.region_17.19_spmd.sunk | while | flops 1536195072 | bytes 170713200 | solution.py:313
  400.6 6.7 %multiply_reduce_fusion.6 = (f32[3,512]{1,0:T(4,128)S(1)}, f32[3,512,1536]{2,1,0:T(8,128)}) fusion(f32[3,512,1536]{2,1,0:T(8,128)S(1)} %fusion.220, f32[3,512]{1,0:T(4,128)S(1)} %dynamic-slice_bitcast_fusion.2, bf16[512,3,64]{0,2,1:T(8,128)(2,1)S(1)} %bitcast.166, bf16[1536,3,64]{0,2,1:T(8,128)(2,1)S(1)} %bitcast.162, ...), kind=kOutput, calls=%fused_computation.21.clone.1 | convolution fusion | flops 316144128 | bytes 20459520 | tf_op jit(solution)/shard_map/while/body/eval_jaxpr/qhd,khd->hqk/dot_general | solution.py:74
  407.3 9.4 %multiply_convert_fusion.3 = bf16[3,512,1536]{2,1,0:T(8,128)(2,1)} fusion(f32[3,512,1536]{2,1,0:T(8,128)} %get-tuple-element.368, f32[3,512,1536]{2,1,0:T(8,128)} %copy-done.2, f32[3,512]{1,0:T(4,128)S(1)} %get-tuple-element.369), kind=kLoop, calls=%fused_computation.20.clone.1 | loop fusion | flops 7077888 | bytes 23599104 | tf_op jit(solution)/shard_map/while/body/eval_jaxpr/convert_element_type | solution.py:155
  439.2 6.7 %multiply_reduce_fusion.6 = (f32[3,512]{1,0:T(4,128)S(1)}, f32[3,512,1536]{2,1,0:T(8,128)}) fusion(f32[3,512,1536]{2,1,0:T(8,128)S(1)} %fusion.220, f32[3,512]{1,0:T(4,128)S(1)} %dynamic-slice_bitcast_fusion.2, bf16[512,3,64]{0,2,1:T(8,128)(2,1)S(1)} %bitcast.166, bf16[1536,3,64]{0,2,1:T(8,128)(2,1)S(1)} %bitcast.162, ...), kind=kOutput, calls=%fused_computation.21.clone.1 | convolution fusion | flops 316144128 | bytes 20459520 | tf_op jit(solution)/shard_map/while/body/eval_jaxpr/qhd,khd->hqk/dot_general | solution.py:74
  445.9 9.4 %multiply_convert_fusion.3 = bf16[3,512,1536]{2,1,0:T(8,128)(2,1)} fusion(f32[3,512,1536]{2,1,0:T(8,128)} %get-tuple-element.368, f32[3,512,1536]{2,1,0:T(8,128)} %copy-done.2, f32[3,512]{1,0:T(4,128)S(1)} %get-tuple-element.369), kind=kLoop, calls=%fused_computation.20.clone.1 | loop fusion | flops 7077888 | bytes 23599104 | tf_op jit(solution)/shard_map/while/body/eval_jaxpr/convert_element_type | solution.py:155
  477.8 6.7 %multiply_reduce_fusion.6 = (f32[3,512]{1,0:T(4,128)S(1)}, f32[3,512,1536]{2,1,0:T(8,128)}) fusion(f32[3,512,1536]{2,1,0:T(8,128)S(1)} %fusion.220, f32[3,512]{1,0:T(4,128)S(1)} %dynamic-slice_bitcast_fusion.2, bf16[512,3,64]{0,2,1:T(8,128)(2,1)S(1)} %bitcast.166, bf16[1536,3,64]{0,2,1:T(8,128)(2,1)S(1)} %bitcast.162, ...), kind=kOutput, calls=%fused_computation.21.clone.1 | convolution fusion | flops 316144128 | bytes 20459520 | tf_op jit(solution)/shard_map/while/body/eval_jaxpr/qhd,khd->hqk/dot_general | solution.py:74
  484.5 9.4 %multiply_convert_fusion.3 = bf16[3,512,1536]{2,1,0:T(8,128)(2,1)} fusion(f32[3,512,1536]{2,1,0:T(8,128)} %get-tuple-element.368, f32[3,512,1536]{2,1,0:T(8,128)} %copy-done.2, f32[3,512]{1,0:T(4,128)S(1)} %get-tuple-element.369), kind=kLoop, calls=%fused_computation.20.clone.1 | loop fusion | flops 7077888 | bytes 23599104 | tf_op jit(solution)/shard_map/while/body/eval_jaxpr/convert_element_type | solution.py:155
  493.9 4.9 fusion.221
  516.3 6.7 %multiply_reduce_fusion.6 = (f32[3,512]{1,0:T(4,128)S(1)}, f32[3,512,1536]{2,1,0:T(8,128)}) fusion(f32[3,512,1536]{2,1,0:T(8,128)S(1)} %fusion.220, f32[3,512]{1,0:T(4,128)S(1)} %dynamic-slice_bitcast_fusion.2, bf16[512,3,64]{0,2,1:T(8,128)(2,1)S(1)} %bitcast.166, bf16[1536,3,64]{0,2,1:T(8,128)(2,1)S(1)} %bitcast.162, ...), kind=kOutput, calls=%fused_computation.21.clone.1 | convolution fusion | flops 316144128 | bytes 20459520 | tf_op jit(solution)/shard_map/while/body/eval_jaxpr/qhd,khd->hqk/dot_general | solution.py:74
  523.1 9.4 %multiply_convert_fusion.3 = bf16[3,512,1536]{2,1,0:T(8,128)(2,1)} fusion(f32[3,512,1536]{2,1,0:T(8,128)} %get-tuple-element.368, f32[3,512,1536]{2,1,0:T(8,128)} %copy-done.2, f32[3,512]{1,0:T(4,128)S(1)} %get-tuple-element.369), kind=kLoop, calls=%fused_computation.20.clone.1 | loop fusion | flops 7077888 | bytes 23599104 | tf_op jit(solution)/shard_map/while/body/eval_jaxpr/convert_element_type | solution.py:155
  532.4 4.9 fusion.221
  552.6 7.9 %add_convert_fusion = bf16[2048,768]{1,0:T(8,128)(2,1)} fusion(f32[2048,768]{1,0:T(8,128)} %fusion.133, f32[2048,768]{1,0:T(8,128)S(1)} %fusion.125, f32[2048,768]{1,0:T(8,128)S(1)} %fusion.132, f32[2048,768]{1,0:T(8,128)S(1)} %fusion.62, f32[2048,8]{0,1:T(8,128)S(1)} %convolution_multiply_fusion.4, bf16[768,8]{0,1:T(8,128)(2,1)S(1)} %copy-done.40), kind=kOutput, calls=%fused_computation.50 | convolution fusion | flops 158859264 | bytes 28389376 | tf_op jit(solution)/shard_map/dot_general | solution.py:334
  570.4 37.0 %all-reduce.3 = (f32[8,3,64]{2,1,0:T(4,128)S(1)}, f32[8,3,64]{2,1,0:T(4,128)S(1)}) all-reduce(f32[8,3,64]{2,1,0:T(4,128)S(1)} %reshape.273, f32[8,3,64]{2,1,0:T(4,128)S(1)} %reshape.274), channel_id=2, replica_groups=mesh['dp'=8,'tensor'=4] {'dp'}, use_global_device_ids=true, to_apply=%region_21.22.clone | all-reduce | flops 3072 | bytes 24576
  608.7 20.5 %all-reduce.15.cloned.1.call-done = bf16[2048,768]{1,0:T(8,128)(2,1)} async-done(((bf16[2048,768]{1,0:T(8,128)(2,1)}), bf16[2048,768]{1,0:T(8,128)(2,1)}) %all-reduce.15.cloned.1.call-update) | async-done | bytes 3145744 | tf_op jit(solution)/shard_map/psum | solution.py:340
  (338 shorter events, 202.0 us)
Async XLA Ops:
  7.2 160.8 %copy-start = (bf16[768,768]{1,0:T(8,128)(2,1)S(1)}, bf16[768,768]{1,0:T(8,128)(2,1)}, u32[]{:S(2)}) copy-start(bf16[768,768]{1,0:T(8,128)(2,1)} %param.25) | copy-start | bytes 3538948
  7.2 9.6 %copy-start.36 = (bf16[768,192]{0,1:T(8,128)(2,1)S(1)}, bf16[768,192]{0,1:T(8,128)(2,1)}, u32[]{:S(2)}) copy-start(bf16[768,192]{0,1:T(8,128)(2,1)} %param.22) | copy-start | bytes 884740
  7.2 151.9 %all-reduce.9.cloned.1.call-start = ((), (), s32[]{:S(2)}) async-start(), calls=%async_computation | async-start | bytes 6291456 | tf_op jit(solution)/shard_map/psum | solution.py:255
  9.0 11.1 %copy-start.44 = (bf16[8,192]{1,0:T(8,128)(2,1)}, bf16[8,192]{1,0:T(8,128)(2,1)S(1)}, u32[]{:S(2)}) copy-start(bf16[8,192]{1,0:T(8,128)(2,1)S(1)} %reshape.272) | copy-start | bytes 9220
  9.8 8.2 %copy-start.46 = (bf16[8,192]{1,0:T(8,128)(2,1)}, bf16[8,192]{1,0:T(8,128)(2,1)S(1)}, u32[]{:S(2)}) copy-start(bf16[8,192]{1,0:T(8,128)(2,1)S(1)} %reshape.269) | copy-start | bytes 9220
  9.8 7.0 %copy-start.4 = (bf16[2048,768]{1,0:T(8,128)(2,1)S(1)}, bf16[2048,768]{1,0:T(8,128)(2,1)}, u32[]{:S(2)}) copy-start(bf16[2048,768]{1,0:T(8,128)(2,1)} %param.19) | copy-start | bytes 9437188
  82.3 80.7 %copy-start.17 = (bf16[3072,192]{0,1:T(8,128)(2,1)}, bf16[3072,192]{0,1:T(8,128)(2,1)S(1)}, u32[]{:S(2)}) copy-start(bf16[3072,192]{0,1:T(8,128)(2,1)S(1)} %get-tuple-element.479) | copy-start | bytes 3538948
  82.3 80.7 %copy-start.18 = (bf16[3072,192]{0,1:T(8,128)(2,1)}, bf16[3072,192]{0,1:T(8,128)(2,1)S(1)}, u32[]{:S(2)}) copy-start(bf16[3072,192]{0,1:T(8,128)(2,1)S(1)} %get-tuple-element.480) | copy-start | bytes 3538948
  87.8 77.6 %copy-start.38 = (f32[768]{0:T(1024)S(1)}, f32[768]{0:T(1024)}, u32[]{:S(2)}) copy-start(f32[768]{0:T(1024)} %param.27) | copy-start | bytes 9220
  87.8 168.8 %all-reduce.11.cloned.1.call-start = ((), (), s32[]{:S(2)}) async-start(), calls=%async_computation.1 | async-start | bytes 6291456 | tf_op jit(solution)/shard_map/psum | solution.py:262
  187.9 68.7 %copy-start.33 = (f32[2048]{0:T(1024)S(1)}, f32[2048]{0:T(1024)}, u32[]{:S(2)}) copy-start(f32[2048]{0:T(1024)} %copy-done.32) | copy-start | bytes 24580
  187.9 180.8 %all-reduce.13.cloned.1.call-start = ((), (), s32[]{:S(2)}) async-start(), calls=%async_computation.2 | async-start | bytes 6291456 | tf_op jit(solution)/shard_map/psum | solution.py:276
  300.0 329.2 %all-reduce.15.cloned.1.call-start = ((), (), s32[]{:S(2)}) async-start(), calls=%async_computation.3 | async-start | bytes 6291456 | tf_op jit(solution)/shard_map/psum | solution.py:340
  368.7 8.4 %copy-start.7 = (bf16[2048,768]{1,0:T(8,128)(2,1)S(1)}, bf16[2048,768]{1,0:T(8,128)(2,1)}, u32[]{:S(2)}) copy-start(bf16[2048,768]{1,0:T(8,128)(2,1)} %param.19) | copy-start | bytes 9437188
  368.7 8.4 %copy-start.10 = (bf16[2048,768]{1,0:T(8,128)(2,1)S(1)}, bf16[2048,768]{1,0:T(8,128)(2,1)}, u32[]{:S(2)}) copy-start(bf16[2048,768]{1,0:T(8,128)(2,1)} %all-reduce.9.cloned.1.call-done) | copy-start | bytes 9437188
  368.7 8.4 %copy-start.26 = (bf16[2048,768]{1,0:T(8,128)(2,1)S(1)}, bf16[2048,768]{1,0:T(8,128)(2,1)}, u32[]{:S(2)}) copy-start(bf16[2048,768]{1,0:T(8,128)(2,1)} %all-reduce.13.cloned.1.call-done) | copy-start | bytes 9437188
  388.6 154.5 %copy-start.47 = (bf16[8,192]{1,0:T(8,128)(2,1)S(1)}, bf16[8,192]{1,0:T(8,128)(2,1)}, u32[]{:S(2)}) copy-start(bf16[8,192]{1,0:T(8,128)(2,1)} %copy-done.46) | copy-start | bytes 9220
  416.7 6.8 %copy-start.23 = (bf16[512,192]{0,1:T(8,128)(2,1)S(1)}, bf16[512,192]{0,1:T(8,128)(2,1)}, u32[]{:S(2)}) copy-start(bf16[512,192]{0,1:T(8,128)(2,1)} %copy-done.22) | copy-start | bytes 589828 | tf_op jit(solution)/shard_map/while
  455.3 6.8 %copy-start.23 = (bf16[512,192]{0,1:T(8,128)(2,1)S(1)}, bf16[512,192]{0,1:T(8,128)(2,1)}, u32[]{:S(2)}) copy-start(bf16[512,192]{0,1:T(8,128)(2,1)} %copy-done.22) | copy-start | bytes 589828 | tf_op jit(solution)/shard_map/while
  493.9 6.8 %copy-start.23 = (bf16[512,192]{0,1:T(8,128)(2,1)S(1)}, bf16[512,192]{0,1:T(8,128)(2,1)}, u32[]{:S(2)}) copy-start(bf16[512,192]{0,1:T(8,128)(2,1)} %copy-done.22) | copy-start | bytes 589828 | tf_op jit(solution)/shard_map/while
  532.4 6.8 %copy-start.23 = (bf16[512,192]{0,1:T(8,128)(2,1)S(1)}, bf16[512,192]{0,1:T(8,128)(2,1)}, u32[]{:S(2)}) copy-start(bf16[512,192]{0,1:T(8,128)(2,1)} %copy-done.22) | copy-start | bytes 589828 | tf_op jit(solution)/shard_map/while
  552.5 8.7 %copy-start.49 = (u32[32]{0:T(128)S(1)}, u32[32]{0:T(128)}, u32[]{:S(2)}) copy-start(u32[32]{0:T(128)} %constant.161) | copy-start | bytes 388
  552.5 10.0 %copy-start.43 = (f32[768]{0:T(1024)S(1)}, f32[768]{0:T(1024)}, u32[]{:S(2)}) copy-start(f32[768]{0:T(1024)} %param.28) | copy-start | bytes 9220
  552.6 79.5 %copy-start.1 = (bf16[768,768]{1,0:T(8,128)(2,1)S(1)}, bf16[768,768]{1,0:T(8,128)(2,1)}, u32[]{:S(2)}) copy-start(bf16[768,768]{1,0:T(8,128)(2,1)} %param.25) | copy-start | bytes 3538948
  (57 other events, 223.3 us)
Sparse Core Ops, SparseCore 0:
  87.9 71.1 all-reduce.8
  188.0 68.5 all-reduce.10
  300.1 68.5 all-reduce.12
  560.6 68.5 all-reduce.14
where the time goes:
time: 649 us; the launch traced here: 639 us
  waiting for transfers between devices  221 us (34%)
  matrix products  173 us (27%)
  other arithmetic  109 us (17%)
  local copies, waits for them, and re-layouts  70.4 us (11%)
  blocking collectives  37 us (6%)
  between operations  15.5 us (2%)
  loops' own time  12.2 us (2%)
    psum x1, waiting for transfers between devices, on_device(): lax.psum(jnp.dot(context, w_out, preferred_element_type=jnp.float32).asty...  71 us
    psum x1, waiting for transfers between devices, on_device(): lax.psum(transpose_dot(grad_pre, w_inner).astype(jnp.bfloat16), 'tensor')  68.6 us
    psum x1, waiting for transfers between devices, on_device(): lax.psum(jnp.dot(active, w_ffn_out, preferred_element_type=jnp.float32).a...  61.1 us
    convert_element_type x4, other arithmetic, attend_backward(): grad_scores = (probability * (grad_prob - row_delta)).astype(jnp.bfloat16)  37.5 us
    unnamed x1, blocking collectives  37 us
    dot_general x8, matrix products, block_scores(): jnp.einsum('qhd,khd->hqk', query_block, key_block, preferred_element_type...  34.9 us
    dot_general x7, matrix products, transpose_dot(): lax.dot_general(left_side, right_side, (((1,), (1,)), ((), ())), preferre...  30 us
    psum x1, waiting for transfers between devices, on_device(): lax.psum(input_term.astype(jnp.bfloat16), 'tensor').astype(jnp.float32)  20.5 us
  transfers between devices with their start and end apart: 4, of which 4 were waited for; matrix products, arithmetic and copies ran while one was open for 3% of the time, Pallas kernels for 0%

commit v1 on v0

v1 whole, which is shorter than its diff:
```python
import functools

import jax
import jax.numpy as jnp
from jax import lax
from jax.experimental import pallas as pl
from jax.experimental.pallas import tpu as pltpu
from jax.sharding import PartitionSpec as P

EPSILON = 1e-05
BLOCKED = -1e30
LOG2E = 1.4426950408889634
BLK = 256
LANES = 128
f32 = jnp.float32
bf16 = jnp.bfloat16
VMEM_LIMIT = 64 * 1024 * 1024 - 65536


def dot(a, b):
    return jnp.dot(a, b, preferred_element_type=f32)


def dot_nt(a, b):
    return lax.dot_general(a, b, (((1,), (1,)), ((), ())), preferred_element_type=f32)


def lane_iota(rows, lanes=LANES):
    return lax.broadcasted_iota(jnp.int32, (rows, lanes), 1)


def selection(rows, lanes, target):
    r = lax.broadcasted_iota(jnp.int32, (rows, lanes), 0)
    c = lax.broadcasted_iota(jnp.int32, (rows, lanes), 1)
    return jnp.where(c == target(r), 1.0, 0.0).astype(bf16)


def three_parts(x):
    hi = x.astype(bf16).astype(f32)
    mid = (x - hi).astype(bf16).astype(f32)
    low = (x - hi - mid).astype(bf16).astype(f32)
    return hi, mid, low


def segment_bounds(len_ref, slots):
    starts, ends = [], []
    total = jnp.int32(0)
    for s in range(slots):
        starts.append(total)
        total = total + len_ref[0, s]
        ends.append(total)
    return starts, ends


def block_range(starts, ends, row0):
    first, last = jnp.int32(0), jnp.int32(0)
    for s, e in zip(starts, ends):
        first = jnp.where((s <= row0) & (row0 < e), s, first)
        edge = row0 + BLK - 1
        last = jnp.where((s <= edge) & (edge < e), e, last)
    return first // BLK, (last + BLK - 1) // BLK


def attend_kernel(heads, hd, len_ref, tok_ref, wq_ref, wk_ref, wv_ref, dq_ref, dv_ref, uq_ref, uv_ref,
                  qa_ref, ka_ref, va_ref, kt_ref, ctx_ref, lowt_ref, weff_ref,
                  wbig, up, scores, peak, total):
    rows = tok_ref.shape[0]
    width = heads * hd
    pad = heads * LANES
    slots = len_ref.shape[1]
    rank = dq_ref.shape[1]
    starts, ends = segment_bounds(len_ref, slots)

    spread = selection(width, pad, lambda r: (r // hd) * LANES + r % hd)
    wq, wk, wv = wq_ref[...], wk_ref[...], wv_ref[...]
    for i, w in enumerate((wq, wk, wv)):
        wbig[:, i * pad:(i + 1) * pad] = dot(w, spread).astype(bf16)
    low_q = selection(rank, LANES, lambda r: r)
    low_v = selection(rank, LANES, lambda r: r + rank)
    wbig[:, 3 * pad:] = (dot(dq_ref[...], low_q) + dot(dv_ref[...], low_v)).astype(bf16)
    uq, uv = uq_ref[...], uv_ref[...]
    up[...] = jnp.zeros_like(up)
    up[0:2 * rank, 0:pad] = dot(selection(2 * rank, rank, lambda r: r), 2.0 * dot(uq, spread).astype(bf16)).astype(bf16)
    up[0:2 * rank, pad:] = dot(selection(2 * rank, rank, lambda r: r - rank), 2.0 * dot(uv, spread).astype(bf16)).astype(bf16)
    pack = weff_ref.shape[1]
    weff_ref[...] = (
        dot((wq.astype(f32) + 2.0 * dot(dq_ref[...], uq)).astype(bf16), selection(width, pack, lambda r: r))
        + dot(wk, selection(width, pack, lambda r: r + width))
        + dot((wv.astype(f32) + 2.0 * dot(dv_ref[...], uv)).astype(bf16), selection(width, pack, lambda r: r + 2 * width))
    ).astype(bf16)

    lane = lane_iota(1)
    seg_start = jnp.zeros((1, LANES), jnp.int32)
    seg_end = jnp.zeros((1, LANES), jnp.int32)
    for s in range(slots):
        seg_start = jnp.where(lane == hd + s, starts[s], seg_start)
        seg_end = jnp.where(lane == hd + s, ends[s], seg_end)
    is_mask = (lane >= hd) & (lane < hd + slots)
    extra = (lane >= hd + slots) & (lane < hd + slots + 3)
    ones_v = jnp.where((lane >= hd) & (lane < hd + 3), 1.0, 0.0)

    def project(i, _):
        r0 = pl.multiple_of(i * BLK, BLK)
        span = pl.ds(r0, BLK)
        x = tok_ref[span, :]
        low = dot(x, wbig[:, 3 * pad:]).astype(bf16)
        lowt_ref[:, span] = low.astype(f32).T[0:2 * rank, :].astype(bf16)
        pos = r0 + lax.broadcasted_iota(jnp.int32, (BLK, LANES), 0)
        own = (pos >= seg_start) & (pos < seg_end)
        q_mask = jnp.where(own, 1.0, 0.0)
        k_mask = jnp.where(is_mask & jnp.logical_not(own), BLOCKED, jnp.where(extra, 1.0, 0.0))
        q = dot(x, wbig[:, 0:pad]) + dot(low, up[:, 0:pad])
        for h in range(heads):
            qh = q[:, h * LANES:(h + 1) * LANES].astype(bf16).astype(f32)
            qa_ref[h, span, :] = (qh * hd ** -0.5 + q_mask).astype(bf16)
        k = dot(x, wbig[:, pad:2 * pad])
        for h in range(heads):
            kh = k[:, h * LANES:(h + 1) * LANES]
            ka_ref[h, span, :] = (kh + k_mask).astype(bf16)
            kt_ref[h, :, span] = kh.T[0:hd, :].astype(bf16)
        v = dot(x, wbig[:, 2 * pad:3 * pad]) + dot(low, up[:, pad:])
        for h in range(heads):
            va_ref[h, span, :] = (v[:, h * LANES:(h + 1) * LANES] + ones_v).astype(bf16)
        return 0

    lax.fori_loop(0, rows // BLK, project, 0)

    lanes = lane_iota(BLK)
    group = ctx_ref.shape[1] * 2 // 3

    def attend(g, half):
        per = group // BLK
        row0 = pl.multiple_of(g * group + half * BLK, BLK)
        span = pl.ds(row0, BLK)
        lo, hi = block_range(starts, ends, row0)
        peak[...] = jnp.full(peak.shape, BLOCKED, f32)
        total[...] = jnp.zeros_like(total)

        def first(kb, _):
            keys = pl.ds(pl.multiple_of(kb * BLK, BLK), BLK)
            for h in range(heads):
                s = dot_nt(qa_ref[h, span, :], ka_ref[h, keys, :])
                scores[h, kb - lo] = s
                best = peak[h]
                for c in range(BLK // LANES):
                    best = jnp.maximum(best, s[:, c * LANES:(c + 1) * LANES])
                peak[h] = best
            return 0

        lax.fori_loop(lo, hi, first, 0)
        for h in range(heads):
            peak[h] = jnp.broadcast_to(jnp.max(peak[h], axis=1, keepdims=True), (BLK, LANES))

        def second(kb, _):
            keys = pl.ds(pl.multiple_of(kb * BLK, BLK), BLK)
            for h in range(heads):
                top = jnp.concatenate([peak[h]] * (BLK // LANES), axis=1)
                p = jnp.exp2((scores[h, kb - lo] - top) * LOG2E).astype(bf16)
                total[h] += dot(p, va_ref[h, keys, :])
            return 0

        lax.fori_loop(lo, hi, second, 0)
        outs = []
        for h in range(heads):
            acc = total[h]
            norm = jnp.broadcast_to(acc[:, hd:hd + 1], (BLK, LANES))
            outs.append(acc / norm)
            hi_p, mid_p, low_p = three_parts(-(peak[h] + jnp.log(norm)))
            old = qa_ref[h, span, :].astype(f32)
            new = jnp.where(lanes == hd + slots, hi_p, old)
            new = jnp.where(lanes == hd + slots + 1, mid_p, new)
            new = jnp.where(lanes == hd + slots + 2, low_p, new)
            qa_ref[h, span, :] = new.astype(bf16)
        pair = jnp.where(lanes < hd, outs[0], pltpu.roll(outs[1], hd, 1))
        ctx_ref[g, half * BLK:(half + 1) * BLK, :] = pair.astype(bf16)
        if half == 0:
            ctx_ref[g, group:group + BLK, :] = outs[2].astype(bf16)
        else:
            both = jnp.where(lanes < hd, ctx_ref[g, group:group + BLK, :].astype(f32), pltpu.roll(outs[2], hd, 1))
            ctx_ref[g, group:group + BLK, :] = both.astype(bf16)

    def attend_group(g, _):
        attend(g, 0)
        attend(g, 1)
        return 0

    lax.fori_loop(0, rows // group, attend_group, 0)


def attend_back_kernel(heads, hd, len_ref, qa_ref, ka_ref, va_ref, kt_ref, ctx_ref, gctx_ref, lowt_ref,
                       g_ref, adp_ref, doa, dk, dv, dqt, dqs):
    rows = qa_ref.shape[1]
    slots = len_ref.shape[1]
    starts, ends = segment_bounds(len_ref, slots)
    dk[...] = jnp.zeros_like(dk)
    dv[...] = jnp.zeros_like(dv)
    lanes = lane_iota(BLK)
    left = lanes < hd
    group = ctx_ref.shape[1] * 2 // 3

    def back(g, half):
        row0 = pl.multiple_of(g * group + half * BLK, BLK)
        span = pl.ds(row0, BLK)
        lo, hi = block_range(starts, ends, row0)
        pair = gctx_ref[g, half * BLK:(half + 1) * BLK, :].astype(f32)
        last = gctx_ref[g, group:group + BLK, :].astype(f32)
        p_pair = pair * ctx_ref[g, half * BLK:(half + 1) * BLK, :].astype(f32)
        p_last = last * ctx_ref[g, group:group + BLK, :].astype(f32)
        deltas = [
            jnp.sum(jnp.where(left, p_pair, 0.0), axis=1, keepdims=True),
            jnp.sum(jnp.where(left, 0.0, p_pair), axis=1, keepdims=True),
            jnp.sum(jnp.where(left, p_last, 0.0) if half == 0 else jnp.where(left, 0.0, p_last), axis=1, keepdims=True),
        ]
        values = [pair, pltpu.roll(pair, hd, 1), last if half == 0 else pltpu.roll(last, hd, 1)]
        for h in range(heads):
            parts = three_parts(-jnp.broadcast_to(deltas[h], (BLK, LANES)))
            d = jnp.where(left, values[h], 0.0)
            for i, part in enumerate(parts):
                d = jnp.where(lanes == hd + i, part, d)
            doa[h] = d.astype(bf16)
        dqt[...] = jnp.zeros_like(dqt)

        def step(kb, _):
            keys = pl.ds(pl.multiple_of(kb * BLK, BLK), BLK)
            for h in range(heads):
                s = dot_nt(ka_ref[h, keys, :], qa_ref[h, span, :])
                p = jnp.exp2(s * LOG2E)
                dp = dot_nt(va_ref[h, keys, :], doa[h])
                ds = (p * dp).astype(bf16)
                dv[h, keys, :] += dot(p.astype(bf16), doa[h])
                dk[h, keys, :] += dot(ds, qa_ref[h, span, :])
                dqt[h * hd:(h + 1) * hd, :] += dot(kt_ref[h, :, keys], ds)
            return 0

        lax.fori_loop(lo, hi, step, 0)
        dqs[span, :] = (dqt[...].T * hd ** -0.5)

    def back_group(g, _):
        back(g, 0)
        back(g, 1)
        return 0

    lax.fori_loop(0, rows // group, back_group, 0)
    adp_ref[...] = jnp.zeros_like(adp_ref)

    def finish(i, _):
        span = pl.ds(pl.multiple_of(i * BLK, BLK), BLK)

        def pair(a, b):
            return jnp.where(left, a, pltpu.roll(b, hd, 1)).astype(bf16)

        g_ref[span, 0:LANES] = dqs[span, 0:LANES].astype(bf16)
        g_ref[span, LANES:2 * LANES] = pair(dqs[span, LANES:2 * LANES], dk[0, span, :])
        g_ref[span, 2 * LANES:3 * LANES] = pair(dk[1, span, :], dk[2, span, :])
        g_ref[span, 3 * LANES:4 * LANES] = pair(dv[0, span, :], dv[1, span, :])
        g_ref[span, 4 * LANES:5 * LANES] = pair(dv[2, span, :], jnp.zeros((BLK, LANES), f32))
        adp_ref[...] += 2.0 * dot(lowt_ref[:, span], g_ref[span, :])
        return 0

    lax.fori_loop(0, rows // BLK, finish, 0)


def phi_parts(a):
    z = jnp.abs(a)
    t = 1.0 / (1.0 + 0.23164188 * z)
    e = jnp.exp2(a * a * (-0.5 * LOG2E))
    q = t * (0.127414796 + t * (-0.142248368 + t * (0.710706871 + t * (-0.726576014 + t * 0.530702714))))
    tail = q * e
    return jnp.where(a >= 0.0, 1.0 - tail, tail), e


def peers(t):
    return (t, t + 1 - 2 * lax.rem(t, 2), lax.rem(t + 2, 4), 3 - t)


def middle_kernel(hd, len_ref, ctx_ref, tok_ref, cot_ref, ow_ref, owy_ref, fi_ref, fiy_ref, fo_ref, foy_ref,
                  g1_ref, g2_ref, act_ref, gmix_ref, gctx_ref,
                  xin, xb, wout, wfi, wfo, tokr, cotr, normed, unit1, inv1, low, acc, gel, gsend, grecv,
                  wsem_s, wsem_r, lsem, csem_s, csem_r, gsem_s, gsem_r):
    me = lax.axis_index("tensor")
    ids = peers(me)
    own = tokr.shape[0]
    feat = tokr.shape[1]
    part = ow_ref.shape[0]
    half = own // 2

    def there(s):
        return {"tensor": ids[s]}

    barrier = pltpu.get_barrier_semaphore()
    for s in (1, 2, 3):
        pl.semaphore_signal(barrier, inc=1, device_id=there(s), device_id_type=pl.DeviceIdType.MESH)
    pl.semaphore_wait(barrier, 3)

    ctx_copies = []
    for s in (2, 3, 1):
        ctx_copies.append([
            pltpu.make_async_remote_copy(
                src_ref=ctx_ref.at[ids[s]], dst_ref=xb.at[s], send_sem=csem_s.at[s], recv_sem=csem_r.at[s],
                device_id=there(s), device_id_type=pl.DeviceIdType.MESH), s])
        ctx_copies[-1][0].start()
    ctx_own = pltpu.make_async_copy(ctx_ref.at[me], xb.at[0], lsem.at[0])
    ctx_own.start()
    rows = pl.ds(pl.multiple_of(me * own, own), own)
    tok_copy = pltpu.make_async_copy(tok_ref.at[rows], tokr, lsem.at[1])
    tok_copy.start()
    cot_copy = pltpu.make_async_copy(cot_ref.at[rows], cotr, lsem.at[2])
    cot_copy.start()
    local, remote = [], []
    for i, (src, srcy, dst) in enumerate(((ow_ref, owy_ref, wout), (fi_ref, fiy_ref, wfi), (fo_ref, foy_ref, wfo))):
        for j, (ref, mine, theirs) in enumerate(((src, 0, 1), (srcy, 2, 3))):
            n = 2 * i + j
            if i == 0:
                to_mine, to_theirs = dst.at[mine, 0:part], dst.at[theirs, 0:part]
            else:
                to_mine, to_theirs = dst.at[mine], dst.at[theirs]
            c = pltpu.make_async_copy(ref, to_mine, lsem.at[3 + n])
            r = pltpu.make_async_remote_copy(
                src_ref=ref, dst_ref=to_theirs, send_sem=wsem_s.at[n], recv_sem=wsem_r.at[n],
                device_id=there(1), device_id_type=pl.DeviceIdType.MESH)
            c.start()
            r.start()
            local.append(c)
            remote.append(r)
    padrows = wout.shape[1] - part
    for s in range(4):
        wout[s, part:, :] = jnp.zeros((padrows, feat), bf16)

    for n in (0, 1):
        local[n].wait()
        remote[n].wait_recv()
    ctx_own.wait()
    tok_copy.wait()
    cot_copy.wait()
    for c, s in ctx_copies:
        c.wait_recv()

    lanes = lane_iota(half)
    for s in range(4):
        xin[:, s * 2 * LANES:s * 2 * LANES + LANES] = xb[s, 0:own, :]
        b = xb[s, own:, :]
        xin[0:half, s * 2 * LANES + LANES:(s + 1) * 2 * LANES] = b
        xin[half:, s * 2 * LANES + LANES:(s + 1) * 2 * LANES] = pltpu.roll(b.astype(f32), hd, 1).astype(bf16)

    wflat = wout.reshape(4 * 2 * LANES, feat)
    acc[...] = dot(xin[...], wflat[...])
    CH = 64
    n_valid = jnp.int32(0)
    for s in range(len_ref.shape[1] - 1):
        n_valid = n_valid + len_ref[0, s]
    g1 = g1_ref[...]
    g2 = g2_ref[...]

    def norm_one(i, _):
        sp = pl.ds(pl.multiple_of(i * CH, CH), CH)
        v = tokr[sp, :].astype(f32) + acc[sp, :]
        mean = jnp.mean(v, axis=-1, keepdims=True)
        c = v - mean
        inv = lax.rsqrt(jnp.mean(c * c, axis=-1, keepdims=True) + EPSILON)
        u = c * inv
        unit1[sp, :] = u
        inv1[sp, :] = jnp.broadcast_to(inv, (CH, LANES))
        nrm = u * g1
        normed[sp, :] = nrm
        low[sp, :] = nrm.astype(bf16)
        return 0

    lax.fori_loop(0, own // CH, norm_one, 0)

    for s in (0, 2, 1, 3):
        n_in, n_out = {0: (2, 4), 2: (3, 5), 1: (2, 4), 3: (3, 5)}[s]
        if s in (0, 2):
            local[n_in].wait()
            local[n_out].wait()
        else:
            remote[n_in].wait_recv()
            remote[n_out].wait_recv()

        for r in range(0, own, BLK):
            pre = dot(low[r:r + BLK, :], wfi[s])
            cdf, e = phi_parts(pre)
            gel[s, r:r + BLK, :] = (cdf + pre * e * 0.3989422804014327).astype(bf16)
            out = dot((pre * cdf).astype(bf16), wfo[s])
            if s == 0:
                acc[r:r + BLK, :] = out
            else:
                acc[r:r + BLK, :] += out

    def norm_two(i, _):
        sp = pl.ds(pl.multiple_of(i * CH, CH), CH)
        v = normed[sp, :] + acc[sp, :]
        mean = jnp.mean(v, axis=-1, keepdims=True)
        c = v - mean
        inv = lax.rsqrt(jnp.mean(c * c, axis=-1, keepdims=True) + EPSILON)
        u = c * inv
        pos = me * own + i * CH + lax.broadcasted_iota(jnp.int32, (CH, 1), 0)
        valid = jnp.where(pos < n_valid, 1.0, 0.0)
        act_ref[sp, :] = (u * g2 * valid).astype(bf16)
        w = cotr[sp, :].astype(f32) * valid * g2
        gm = inv * (w - jnp.mean(w, axis=-1, keepdims=True) - u * jnp.mean(w * u, axis=-1, keepdims=True))
        acc[sp, :] = gm
        low[sp, :] = gm.astype(bf16)
        return 0

    lax.fori_loop(0, own // CH, norm_two, 0)

    for s in range(4):
        for r in range(0, own, BLK):
            ga = dot_nt(low[r:r + BLK, :], wfo[s])
            gp = (ga * gel[s, r:r + BLK, :].astype(f32)).astype(bf16)
            acc[r:r + BLK, :] += dot_nt(gp, wfi[s])

    def norm_back(i, _):
        sp = pl.ds(pl.multiple_of(i * CH, CH), CH)
        w = acc[sp, :] * g1
        u = unit1[sp, :]
        inv = inv1[sp, 0:1]
        gm = inv * (w - jnp.mean(w, axis=-1, keepdims=True) - u * jnp.mean(w * u, axis=-1, keepdims=True))
        gmix_ref[sp, :] = gm
        low[sp, :] = gm.astype(bf16)
        return 0

    lax.fori_loop(0, own // CH, norm_back, 0)

    sends = []
    for s in (2, 3, 1, 0):
        g = dot_nt(low[...], wout[s])
        gsend[s, 0:own, :] = g[:, 0:LANES].astype(bf16)
        b = jnp.where(lanes < hd, g[0:half, LANES:], pltpu.roll(g[half:, LANES:], hd, 1))
        gsend[s, own:, :] = b.astype(bf16)
        if s:
            c = pltpu.make_async_remote_copy(
                src_ref=gsend.at[s], dst_ref=grecv.at[s], send_sem=gsem_s.at[s], recv_sem=gsem_r.at[s],
                device_id=there(s), device_id_type=pl.DeviceIdType.MESH)
            c.start()
            sends.append((c, s))
    outs = [pltpu.make_async_copy(gsend.at[0], gctx_ref.at[me], lsem.at[0])]
    outs[0].start()
    for c, s in sends[::-1]:
        c.wait_recv()
        o = pltpu.make_async_copy(grecv.at[s], gctx_ref.at[ids[s]], lsem.at[s])
        o.start()
        outs.append(o)
    for c, s in sends:
        c.wait_send()
    for c, s in ctx_copies:
        c.wait_send()
    for c in remote:
        c.wait_send()
    for o in outs:
        o.wait()


def last_kernel(n_dp, g_ref, weff_ref, gmix_ref, adp_ref, out_ref, sum_ref,
                gs, wp, psend, precv, asend, arecv,
                ssem, rsem, lsem, psem_s, psem_r, asem_s, asem_r):
    me = lax.axis_index("tensor")
    dp = lax.axis_index("dp")
    ids = peers(me)
    own = out_ref.shape[0]

    def there(s):
        return {"tensor": ids[s]}

    def row(d):
        return {"dp": lax.rem(dp + d, n_dp)}

    barrier = pltpu.get_barrier_semaphore()
    for s in (1, 2):
        pl.semaphore_signal(barrier, inc=1, device_id=there(s), device_id_type=pl.DeviceIdType.MESH)
    for d in range(1, n_dp):
        pl.semaphore_signal(barrier, inc=1, device_id=row(d), device_id_type=pl.DeviceIdType.MESH)
    pl.semaphore_wait(barrier, 2 + n_dp - 1)

    def group(s):
        return g_ref.at[pl.ds(pl.multiple_of(ids[s] * own, own), own)]

    def remote(src, dst, i):
        c = pltpu.make_async_remote_copy(src_ref=src, dst_ref=dst, send_sem=ssem.at[i], recv_sem=rsem.at[i],
                                         device_id=there(1), device_id_type=pl.DeviceIdType.MESH)
        c.start()
        return c

    sent = [remote(group(3), gs.at[0, 1], 0), remote(weff_ref, wp.at[1], 1), remote(group(1), gs.at[1, 1], 2)]
    local = [pltpu.make_async_copy(group(2), gs.at[0, 0], lsem.at[0]),
             pltpu.make_async_copy(weff_ref, wp.at[0], lsem.at[1]),
             pltpu.make_async_copy(group(0), gs.at[1, 0], lsem.at[2])]
    for c in local:
        c.start()
    half = adp_ref.shape[0] // 2
    wide = 2 * LANES
    cols = adp_ref.shape[1]
    asend[:, 0:wide] = adp_ref[0:half, 0:wide]
    asend[:, wide:] = adp_ref[half:, cols - wide:]
    asent = []
    for d in range(1, n_dp):
        c = pltpu.make_async_remote_copy(src_ref=asend, dst_ref=arecv.at[d], send_sem=asem_s.at[d], recv_sem=asem_r.at[d],
                                         device_id=row(d), device_id_type=pl.DeviceIdType.MESH)
        c.start()
        asent.append(c)
    local[0].wait()
    local[1].wait()
    sent[0].wait_recv()
    sent[1].wait_recv()
    psent = []
    for i in range(own // LANES):
        sp = slice(i * LANES, (i + 1) * LANES)
        psend[sp, :] = (dot_nt(gs[0, 0, sp, :], wp[0]) + dot_nt(gs[0, 1, sp, :], wp[1])).astype(bf16)
        c = pltpu.make_async_remote_copy(src_ref=psend.at[sp], dst_ref=precv.at[sp], send_sem=psem_s.at[i],
                                         recv_sem=psem_r.at[i], device_id=there(2), device_id_type=pl.DeviceIdType.MESH)
        c.start()
        psent.append(c)
    local[2].wait()
    sent[2].wait_recv()
    for i in range(own // LANES):
        sp = slice(i * LANES, (i + 1) * LANES)
        out_ref[sp, :] = gmix_ref[sp, :] + (dot_nt(gs[1, 0, sp, :], wp[0]) + dot_nt(gs[1, 1, sp, :], wp[1]))
    total = asend[...]
    for c in asent:
        c.wait_recv()
    for d in range(1, n_dp):
        total = total + arecv[d]
    sum_ref[...] = total
    for i in range(own // LANES):
        sp = slice(i * LANES, (i + 1) * LANES)
        psent[i].wait_recv()
        out_ref[sp, :] += precv[sp, :].astype(f32)
    for c in psent + sent + asent:
        c.wait_send()


def vmem(shape, dtype):
    return pltpu.VMEM(shape, dtype)


V = pl.BlockSpec(memory_space=pltpu.VMEM)
S = pl.BlockSpec(memory_space=pltpu.SMEM)
ANY = pl.BlockSpec(memory_space=pl.ANY)


def on_device(n_dp, groups, tokens, seq_lengths, query_weight, key_weight, value_weight, out_weight, ffn_in, ffn_out,
              gain_attn, gain_ffn, query_down, value_down, query_up, value_up, cotangent):
    rows, feat = tokens.shape
    width = query_weight.shape[1]
    rank, heads, hd = query_up.shape
    hidden = ffn_in.shape[1]
    own = rows // groups
    packed = own + own // 2
    pack = 5 * LANES
    shape = jax.ShapeDtypeStruct
    y_pairs = [(i, i ^ 2) for i in range(groups)]
    out_y = lax.ppermute(out_weight, "tensor", y_pairs)
    fi_y = lax.ppermute(ffn_in, "tensor", y_pairs)
    fo_y = lax.ppermute(ffn_out, "tensor", y_pairs)

    dma = pltpu.SemaphoreType.DMA
    qa, ka, va, kt, ctx, lowt, weff = pl.pallas_call(
        functools.partial(attend_kernel, heads, hd),
        out_shape=(shape((heads, rows, LANES), bf16), shape((heads, rows, LANES), bf16), shape((heads, rows, LANES), bf16),
                   shape((heads, hd, rows), bf16), shape((groups, packed, LANES), bf16), shape((2 * rank, rows), bf16),
                   shape((feat, pack), bf16)),
        in_specs=[S] + [V] * 8,
        out_specs=(V,) * 7,
        scratch_shapes=[vmem((feat, 3 * heads * LANES + LANES), bf16), vmem((LANES, 2 * heads * LANES), bf16),
                        vmem((heads, 5, BLK, BLK), f32), vmem((heads, BLK, LANES), f32), vmem((heads, BLK, LANES), f32)],
        compiler_params=pltpu.CompilerParams(vmem_limit_bytes=VMEM_LIMIT),
        cost_estimate=pl.CostEstimate(flops=20 * 10**9, bytes_accessed=20 * 2**20, transcendentals=4 * 10**6),
        name="attend",
    )(seq_lengths, tokens, query_weight, key_weight, value_weight, query_down, value_down,
      query_up.reshape(rank, width), value_up.reshape(rank, width))

    act, gmix, gctx = pl.pallas_call(
        functools.partial(middle_kernel, hd),
        out_shape=(shape((own, feat), bf16), shape((own, feat), f32), shape((groups, packed, LANES), bf16)),
        in_specs=[S] + [ANY] * 9 + [V] * 2,
        out_specs=(V, V, ANY),
        scratch_shapes=[
            vmem((own, groups * 2 * LANES), bf16), vmem((groups, packed, LANES), bf16), vmem((groups, 2 * LANES, feat), bf16),
            vmem((groups, feat, hidden), bf16), vmem((groups, hidden, feat), bf16), vmem((own, feat), bf16), vmem((own, feat), bf16),
            vmem((own, feat), f32), vmem((own, feat), f32), vmem((own, LANES), f32), vmem((own, feat), bf16), vmem((own, feat), f32),
            vmem((groups, own, hidden), bf16), vmem((groups, packed, LANES), bf16), vmem((groups, packed, LANES), bf16),
            dma((6,)), dma((6,)), dma((9,)), dma((4,)), dma((4,)), dma((4,)), dma((4,))],
        compiler_params=pltpu.CompilerParams(vmem_limit_bytes=VMEM_LIMIT, collective_id=0, has_side_effects=True),
        cost_estimate=pl.CostEstimate(flops=11 * 10**9, bytes_accessed=20 * 2**20, transcendentals=4 * 10**6),
        name="middle",
    )(seq_lengths, ctx, tokens, cotangent, out_weight, out_y, ffn_in, fi_y, ffn_out, fo_y,
      gain_attn.reshape(1, feat), gain_ffn.reshape(1, feat))

    grads, adapter = pl.pallas_call(
        functools.partial(attend_back_kernel, heads, hd),
        out_shape=(shape((rows, pack), bf16), shape((2 * rank, pack), f32)),
        in_specs=[S] + [V] * 7,
        out_specs=(V, V),
        scratch_shapes=[vmem((heads, BLK, LANES), bf16), vmem((heads, rows, LANES), f32), vmem((heads, rows, LANES), f32),
                        vmem((2 * LANES, BLK), f32), vmem((rows, 2 * LANES), f32)],
        compiler_params=pltpu.CompilerParams(vmem_limit_bytes=VMEM_LIMIT),
        cost_estimate=pl.CostEstimate(flops=20 * 10**9, bytes_accessed=20 * 2**20, transcendentals=4 * 10**6),
        name="attend_back",
    )(seq_lengths, qa, ka, va, kt, ctx, gctx, lowt)

    grad_input, adapter_sum = pl.pallas_call(
        functools.partial(last_kernel, n_dp),
        out_shape=(shape((own, feat), f32), shape((rank, 4 * LANES), f32)),
        in_specs=[ANY, ANY, V, V],
        out_specs=(V, V),
        scratch_shapes=[
            vmem((2, 2, own, pack), bf16), vmem((2, feat, pack), bf16), vmem((own, feat), bf16), vmem((own, feat), bf16),
            vmem((rank, 4 * LANES), f32), vmem((n_dp, rank, 4 * LANES), f32),
            dma((3,)), dma((3,)), dma((3,)), dma((4,)), dma((4,)), dma((n_dp,)), dma((n_dp,))],
        compiler_params=pltpu.CompilerParams(vmem_limit_bytes=VMEM_LIMIT, collective_id=1, has_side_effects=True),
        cost_estimate=pl.CostEstimate(flops=2 * 10**9, bytes_accessed=10 * 2**20, transcendentals=0),
        name="last",
    )(grads, weff, gmix, adapter)

    cols = hd // n_dp
    first = lax.axis_index("dp") * cols

    def pick(x):
        return lax.dynamic_slice_in_dim(x.reshape(rank, heads, hd), first, cols, 2)

    up_q = pick(adapter_sum[:, 0:width])
    up_v = pick(adapter_sum[:, 4 * LANES - width - hd:4 * LANES - hd])
    return act, grad_input, up_q, up_v


def solution(mesh):
    in_specs = (
        P("dp", None), P("dp", None), P(None, "tensor"), P(None, "tensor"), P(None, "tensor"), P("tensor", None),
        P(None, "tensor"), P("tensor", None), P(), P(), P(), P(), P(None, "tensor", None), P(None, "tensor", None),
        P("dp", None),
    )
    out_specs = (P(("dp", "tensor"), None), P(("dp", "tensor"), None), P(None, "tensor", "dp"), P(None, "tensor", "dp"))
    return jax.shard_map(
        functools.partial(on_device, mesh.shape["dp"], mesh.shape["tensor"]),
        mesh=mesh, in_specs=in_specs, out_specs=out_specs, check_vma=False,
    )
```

time: 649 us -> 177 us (0.27); the launches traced: 639 us -> 177 us
  waiting for transfers between devices: 221 us -> 10.7 us
  matrix products: 173 us -> 0 us
  Pallas kernels: 0 us -> 144 us
  other arithmetic: 109 us -> 0 us
  local copies, waits for them, and re-layouts: 70.4 us -> 15.7 us
  blocking collectives: 37 us -> 0 us
  between operations: 15.5 us -> 0.71 us
  loops' own time: 12.2 us -> 0 us
    psum x4 -> x0, waiting for transfers between devices: 221 us -> none  [the longest x1 71 us: on_device(): lax.psum(jnp.dot(context, w_out, preferred_element_type=jnp.float32).asty...]
    dot_general x49 -> x0, matrix products: 173 us -> none  [the longest x8 34.9 us: block_scores(): jnp.einsum('qhd,khd->hqk', query_block, key_block, preferred_element_type...]
    pallas_call x0 -> x4, Pallas kernels: none -> 144 us  [the longest x1 46.8 us: on_device(): pl.pallas_call(functools.partial(middle_kernel, hd), out_shape=(shape((ow...]
    convert_element_type x7 -> x0, other arithmetic: 43.2 us -> none  [the longest x4 37.5 us: attend_backward(): grad_scores = (probability * (grad_prob - row_delta)).astype(jnp.bfloat16)]
    reduce_sum x11 -> x0, other arithmetic: 39.6 us -> none  [the longest x2 13 us: normalize_back(): jnp.mean(scaled, axis=-1, keepdims=True)]
    dynamic_slice x53 -> x1, local copies, waits for them, and re-layouts: 38.4 us -> 0.08 us  [pick(): return lax.dynamic_slice_in_dim(x.reshape(rank, heads, hd), first, cols, 2)]
    unnamed x1 -> x0, blocking collectives: 37 us -> none
    another operation x2 -> x0, loops' own time: 12.2 us -> none  [the longest x1 9.72 us: on_device(): lax.scan(back_step, (empty_ext, empty_ext), jnp.arange(block_count))]
  transfers between devices with their start and end apart: 4 -> 3, of which waited for: 4 -> 1; matrix products, arithmetic and copies ran while one was open for 3% -> 6% of each run, Pallas kernels for 0% -> 20%
where the time goes in v1:
time: 177 us
  Pallas kernels  144 us (81%)
  local copies, waits for them, and re-layouts  15.7 us (9%)
  waiting for transfers between devices  10.7 us (6%)
  starting transfers between devices  5.09 us (3%)
    pallas_call x1, Pallas kernels, on_device(): pl.pallas_call(functools.partial(middle_kernel, hd), out_shape=(shape((ow...  46.8 us
    pallas_call x1, Pallas kernels, on_device(): pl.pallas_call(functools.partial(attend_kernel, heads, hd), out_shape=(sh...  35 us
    pallas_call x1, Pallas kernels, on_device(): pl.pallas_call(functools.partial(attend_back_kernel, heads, hd), out_shap...  32.5 us
    pallas_call x1, Pallas kernels, on_device(): pl.pallas_call(functools.partial(last_kernel, n_dp), out_shape=(shape((ow...  30.2 us
    unnamed x23, local copies, waits for them, and re-layouts  10.8 us
    ppermute x1, waiting for transfers between devices, on_device(): out_y = lax.ppermute(out_weight, 'tensor', y_pairs)  10.6 us
  transfers between devices with their start and end apart: 3, of which 1 were waited for; matrix products, arithmetic and copies ran while one was open for 6% of the time, Pallas kernels for 20%

profile of v1, /device:TPU:0, one launch (start us, length us, event | category | flops | bytes accessed | tf_op | source)
XLA Modules:
  0.0 176.7 jit_solution(12908387245514923257)
XLA Ops:
  0.7 3.1 %collective-permute-start.1 = (bf16[768,768]{1,0:T(8,128)(2,1)}, bf16[768,768]{1,0:T(8,128)(2,1)}, u32[]{:S(2)}, u32[]{:S(2)}) collective-permute-start(bf16[768,768]{1,0:T(8,128)(2,1)} %fi_ref.1), channel_id=1, source_target_pairs={{0,2},{1,3},{2,0},{3,1},{4,6},{5,7},{6,4},{7,5},{8,10},{9,11},{10,... | collective-permute-start | bytes 3538952 | tf_op jit(solution)/shard_map/ppermute | solution.py:553
  3.7 0.1 collective-permute-start.2
  3.8 1.9 %collective-permute-start = (bf16[192,768]{1,0:T(8,128)(2,1)}, bf16[192,768]{1,0:T(8,128)(2,1)}, u32[]{:S(2)}, u32[]{:S(2)}) collective-permute-start(bf16[192,768]{1,0:T(8,128)(2,1)} %ow_ref.1), channel_id=1, source_target_pairs={{0,2},{1,3},{2,0},{3,1},{4,6},{5,7},{6,4},{7,5},{8,10},{9,11},{10,... | collective-permute-start | bytes 884744 | tf_op jit(solution)/shard_map/ppermute | solution.py:552
  5.8 1.9 %copy.30.wq_ref = bf16[768,192]{1,0:T(8,128)(2,1)} copy(bf16[768,192]{0,1:T(8,128)(2,1)} %param.17) | data formatting | bytes 589824 | tf_op args[2]
  7.7 1.9 %copy.31.wk_ref = bf16[768,192]{1,0:T(8,128)(2,1)} copy(bf16[768,192]{0,1:T(8,128)(2,1)} %param.18) | data formatting | bytes 589824 | tf_op args[3]
  9.5 0.9 copy.32.wv_ref
  10.5 0.8 copy.33.dq_ref
  11.3 0.8 copy.34.dv_ref
  12.1 0.7 reshape.26.uq_ref
  12.8 0.7 reshape.27.uv_ref
  13.5 35.0 %attend.1 = (bf16[3,2048,128]{2,1,0:T(8,128)(2,1)}, bf16[3,2048,128]{2,1,0:T(8,128)(2,1)}, bf16[3,2048,128]{2,1,0:T(8,128)(2,1)}, bf16[3,64,2048]{2,1,0:T(8,128)...) custom-call(s32[1,9]{1,0:T(1,128)} %len_ref.5, ...), custom_call_target="tpu_custom_call" | custom-call | flops 20000000000 | bytes 20971520 | tf_op jit(solution)/shard_map/attend/pallas_call | solution.py:557
  48.4 1.3 reshape.28.g1_ref
  49.7 1.3 reshape.29.g2_ref
  51.0 10.6 %collective-permute-done.owy_ref = bf16[192,768]{1,0:T(8,128)(2,1)} collective-permute-done((bf16[192,768]{1,0:T(8,128)(2,1)}, bf16[192,768]{1,0:T(8,128)(2,1)}, u32[]{:S(2)}, u32[]{:S(2)}) %collective-permute-start) | collective-permute-done | bytes 294944 | tf_op jit(solution)/shard_map/ppermute | solution.py:552
  61.6 46.8 %middle.1 = (bf16[512,768]{1,0:T(8,128)(2,1)}, f32[512,768]{1,0:T(8,128)}, bf16[4,768,128]{2,1,0:T(8,128)(2,1)}) custom-call(s32[1,9]{1,0:T(1,128)} %len_ref.5, bf16[4,768,128]{2,1,0:T(8,128)(2,1)} %get-tuple-element.18.ctx_ref, bf16[2048,768]{1,0:T(8,128)(2,1)} %tok_ref.3, bf16[2048,768]{1,0:T(8,128)(2,1)} %cot_ref.1, bf16[192,768]{1,0:T(8,128)(2,1)} %ow_ref.1, ...), custom_call_target="tpu_custom_call" | custom-call | flops 11000000512 | bytes 20971520 | tf_op jit(solution)/shard_map/middle/pallas_call | solution.py:572
  108.4 32.5 %attend_back.1 = (bf16[2048,640]{1,0:T(8,128)(2,1)}, f32[16,640]{1,0:T(8,128)}) custom-call(s32[1,9]{1,0:T(1,128)} %len_ref.5, bf16[3,2048,128]{2,1,0:T(8,128)(2,1)} %get-tuple-element.20.qa_ref, bf16[3,2048,128]{2,1,0:T(8,128)(2,1)} %get-tuple-element.21.ka_ref, bf16[3,2048,128]{2,1,0:T(8,128)(2,1)} %get-tuple-element.22.va_ref, ...), custom_call_target="tpu_custom_call" | custom-call | flops 20000000000 | bytes 20971520 | tf_op jit(solution)/shard_map/attend_back/pallas_call | solution.py:589
  140.9 30.2 %last.1 = (f32[512,768]{1,0:T(8,128)}, f32[8,512]{1,0:T(8,128)}) custom-call(bf16[2048,640]{1,0:T(8,128)(2,1)} %get-tuple-element.26.g_ref, bf16[768,640]{1,0:T(8,128)(2,1)} %get-tuple-element.27.weff_ref, f32[512,768]{1,0:T(8,128)} %get-tuple-element.28.gmix_ref, f32[16,640]{1,0:T(8,128)} %get-tuple-element.29.adp_ref), custom_call_target="tpu_custom_call" | custom-call | flops 2000000000 | bytes 10485760 | tf_op jit(solution)/shard_map/last/pallas_call | solution.py:601
  171.2 0.8 fusion
  172.0 0.1 reshape.30
  172.2 0.1 constant_dynamic-slice_fusion
  172.2 0.6 copy.35
  172.9 0.6 copy.36
  173.5 2.1 %copy.39 = bf16[512,768]{1,0:T(8,128)(2,1)} copy(bf16[512,768]{1,0:T(8,128)(2,1)} %get-tuple-element.44) | data formatting | bytes 1572864
  175.5 1.1 copy.40
  (17 shorter events, 0.1 us)
Async XLA Ops:
  0.6 8.9 %copy-start.1 = (bf16[768,192]{0,1:T(8,128)(2,1)S(1)}, bf16[768,192]{0,1:T(8,128)(2,1)}, u32[]{:S(2)}) copy-start(bf16[768,192]{0,1:T(8,128)(2,1)} %param.19) | copy-start | bytes 884740
  0.6 9.8 %copy-start.2 = (bf16[768,8]{0,1:T(8,128)(2,1)S(1)}, bf16[768,8]{0,1:T(8,128)(2,1)}, u32[]{:S(2)}) copy-start(bf16[768,8]{0,1:T(8,128)(2,1)} %param.25) | copy-start | bytes 36868
  0.7 10.6 %copy-start.3 = (bf16[768,8]{0,1:T(8,128)(2,1)S(1)}, bf16[768,8]{0,1:T(8,128)(2,1)}, u32[]{:S(2)}) copy-start(bf16[768,8]{0,1:T(8,128)(2,1)} %param.26) | copy-start | bytes 36868
  0.7 11.4 %copy-start.4 = (bf16[8,3,64]{2,0,1:T(8,128)(2,1)S(1)}, bf16[8,3,64]{2,0,1:T(8,128)(2,1)}, u32[]{:S(2)}) copy-start(bf16[8,3,64]{2,0,1:T(8,128)(2,1)} %param.27) | copy-start | bytes 9220
  0.7 12.1 %copy-start.5 = (bf16[8,3,64]{2,0,1:T(8,128)(2,1)S(1)}, bf16[8,3,64]{2,0,1:T(8,128)(2,1)}, u32[]{:S(2)}) copy-start(bf16[8,3,64]{2,0,1:T(8,128)(2,1)} %param.28) | copy-start | bytes 9220
  0.7 61.0 %collective-permute-start.1 = (bf16[768,768]{1,0:T(8,128)(2,1)}, bf16[768,768]{1,0:T(8,128)(2,1)}, u32[]{:S(2)}, u32[]{:S(2)}) collective-permute-start(bf16[768,768]{1,0:T(8,128)(2,1)} %fi_ref.1), channel_id=1, source_target_pairs={{0,2},{1,3},{2,0},{3,1},{4,6},{5,7},{6,4},{7,5},{8,10},{9,11},{10,... | collective-permute-start | bytes 3538952 | tf_op jit(solution)/shard_map/ppermute | solution.py:553
  3.7 57.9 %collective-permute-start.2 = (bf16[768,768]{1,0:T(8,128)(2,1)}, bf16[768,768]{1,0:T(8,128)(2,1)}, u32[]{:S(2)}, u32[]{:S(2)}) collective-permute-start(bf16[768,768]{1,0:T(8,128)(2,1)} %fo_ref.1), channel_id=1, source_target_pairs={{0,2},{1,3},{2,0},{3,1},{4,6},{5,7},{6,4},{7,5},{8,10},{9,11},{10,... | collective-permute-start | bytes 3538952 | tf_op jit(solution)/shard_map/ppermute | solution.py:554
  3.8 57.8 %collective-permute-start = (bf16[192,768]{1,0:T(8,128)(2,1)}, bf16[192,768]{1,0:T(8,128)(2,1)}, u32[]{:S(2)}, u32[]{:S(2)}) collective-permute-start(bf16[192,768]{1,0:T(8,128)(2,1)} %ow_ref.1), channel_id=1, source_target_pairs={{0,2},{1,3},{2,0},{3,1},{4,6},{5,7},{6,4},{7,5},{8,10},{9,11},{10,... | collective-permute-start | bytes 884744 | tf_op jit(solution)/shard_map/ppermute | solution.py:552
  171.2 4.4 %copy-start = (f32[512,768]{1,0:T(8,128)S(1)}, f32[512,768]{1,0:T(8,128)}, u32[]{:S(2)}) copy-start(f32[512,768]{1,0:T(8,128)} %get-tuple-element.45) | copy-start | bytes 4718596

commit v2 on v0

v2 whole, which is shorter than its diff:
```python
import functools

import jax
import jax.numpy as jnp
from jax import lax
from jax.experimental import pallas as pl
from jax.experimental.pallas import tpu as pltpu
from jax.sharding import PartitionSpec as P

EPSILON = 1e-05
BLOCKED = -1e30
LOG2E = 1.4426950408889634
BLK = 256
HALF = BLK // 2
LANES = 128
REACH = 2
f32 = jnp.float32
bf16 = jnp.bfloat16
VMEM_LIMIT = 64 * 1024 * 1024 - 65536
MESH = pl.DeviceIdType.MESH
TN = (((0,), (0,)), ((), ()))


def dot(a, b):
    return jnp.dot(a, b, preferred_element_type=f32)


def dot_nt(a, b):
    return lax.dot_general(a, b, (((1,), (1,)), ((), ())), preferred_element_type=f32)


def iota(shape, axis):
    return lax.broadcasted_iota(jnp.int32, shape, axis)


def three_parts(x):
    hi = x.astype(bf16).astype(f32)
    mid = (x - hi).astype(bf16).astype(f32)
    low = (x - hi - mid).astype(bf16).astype(f32)
    return hi, mid, low


def phi_parts(a):
    z = jnp.abs(a)
    t = 1.0 / (1.0 + 0.23164188 * z)
    e = jnp.exp2(a * a * (-0.5 * LOG2E))
    q = t * (0.127414796 + t * (-0.142248368 + t * (0.710706871 + t * (-0.726576014 + t * 0.530702714))))
    tail = q * e
    return jnp.where(a >= 0.0, 1.0 - tail, tail), e


def moments(v):
    mean = jnp.mean(v, axis=-1, keepdims=True)
    c = v - mean
    inv = lax.rsqrt(jnp.mean(c * c, axis=-1, keepdims=True) + EPSILON)
    return c * inv, inv


def pull(w, u, inv):
    return inv * (w - jnp.mean(w, axis=-1, keepdims=True) - u * jnp.mean(w * u, axis=-1, keepdims=True))


class Bag:
    pass


def layer_kernel(n_dp, heads, hd, names, *refs):
    z = Bag()
    for name, ref in zip(names, refs):
        setattr(z, name, ref)
    rows, feat = z.tok.shape
    blocks = rows // BLK
    own = z.out.shape[0]
    per = own // BLK
    width = heads * hd
    slots = z.lens.shape[1]
    rank = z.dq.shape[0]
    pack = z.weff.shape[0]
    part = z.ow.shape[0]
    me = lax.axis_index("tensor")
    dp = lax.axis_index("dp")
    yy, cc = lax.div(me, 2), lax.rem(me, 2)
    px, pz = lax.rem(dp, 2), lax.rem(lax.div(dp, 2), 2)

    def member(k):
        fy = 1 - k // 2
        fc = (k % 2 + k // 2) % 2
        return 2 * lax.rem(yy + fy, 2) + lax.rem(cc + fc, 2)

    def tensor_at(k):
        return {"tensor": member(k)}

    x_peer = {"dp": dp + 1 - 2 * px}
    z_peer = {"dp": dp + 2 - 4 * pz}

    def row_at(d):
        return {"dp": lax.rem(dp + d, n_dp)}

    def remote(src, dst, send, recv, device):
        return pltpu.make_async_remote_copy(src_ref=src, dst_ref=dst, send_sem=send, recv_sem=recv,
                                            device_id=device, device_id_type=MESH)

    per_chunk = rows // 4
    tok_in = [pltpu.make_async_copy(z.tok_hbm.at[pl.ds(j * per_chunk, per_chunk)], z.tok.at[pl.ds(j * per_chunk, per_chunk)],
                                    z.lsem.at[j]) for j in range(4)]
    cot_in = pltpu.make_async_copy(z.cot_hbm.at[pl.ds(pl.multiple_of(me * own, own), own)], z.cot, z.lsem.at[4])
    weights = ((z.ow, z.wout), (z.fi, z.wfi), (z.fo, z.wfo))

    def full(dst, k):
        return dst.at[k, 0:part] if dst is z.wout else dst.at[k]

    own_w = [pltpu.make_async_copy(src, full(dst, 3), z.lsem.at[5 + i]) for i, (src, dst) in enumerate(weights)]
    for c in tok_in + own_w + [cot_in]:
        c.start()
    barrier = pltpu.get_barrier_semaphore()
    for k in range(3):
        pl.semaphore_signal(barrier, inc=1, device_id=tensor_at(k), device_id_type=MESH)
    for d in range(1, n_dp):
        pl.semaphore_signal(barrier, inc=1, device_id=row_at(d), device_id_type=MESH)

    z.weff[width:2 * width, :] = z.wk[...]
    for base, w_ref, d_ref, u_ref in ((0, z.wq, z.dq, z.uq), (2 * width, z.wv, z.dv, z.uv)):
        for h in range(heads):
            low_rank = lax.dot_general(u_ref[h], d_ref[...], TN, preferred_element_type=f32)
            mine = w_ref[h * hd:(h + 1) * hd, :].astype(f32) + 2.0 * low_rank
            z.weff[base + h * hd:base + (h + 1) * hd, :] = mine.astype(bf16)
    downs = jnp.concatenate([z.dq[...].astype(f32), z.dv[...].astype(f32)], axis=0)
    z.weff[3 * width:3 * width + 2 * rank, :] = downs.astype(bf16)
    z.weff[3 * width + 2 * rank:, :] = jnp.zeros((pack - 3 * width - 2 * rank, feat), bf16)
    for h in range(heads):
        z.vt[h, hd:, :] = jnp.ones((z.vt.shape[1] - hd, rows), bf16)
    for k in range(4):
        z.wout[k, part:, :] = jnp.zeros((z.wout.shape[1] - part, feat), bf16)
    pl.semaphore_wait(barrier, 3 + n_dp - 1)

    def quarter(dst, k, dx, dz):
        n = (part if dst is z.wout else dst.shape[1]) // 4
        q = 2 * lax.rem(pz + dz, 2) + lax.rem(px + dx, 2)
        return dst.at[k, pl.ds(pl.multiple_of(q * n, n), n)]

    def quarter_of(src):
        n = src.shape[0] // 4
        return src.at[pl.ds(pl.multiple_of((2 * pz + px) * n, n), n)]

    moves = []
    for i, (src, dst) in enumerate(weights):
        v = Bag()
        x_first = i < 2
        sem = lambda j, i=i: (z.wsem_s.at[i, j], z.wsem_r.at[i, j])
        v.a = remote(quarter_of(src), quarter(dst, 0, 0, 0), *sem(0), tensor_at(0))
        v.partner = remote(src, full(dst, 2), *sem(1), tensor_at(2))
        v.x = remote(quarter(dst, 0, 0, 0), quarter(dst, 0, 0, 0), *sem(2), x_peer)
        v.z = remote(quarter(dst, 0, 0, 0), quarter(dst, 0, 0, 0), *sem(3), z_peer)
        far = (1, 0) if x_first else (0, 1)
        v.second = remote(quarter(dst, 0, *far), quarter(dst, 0, *far), *sem(4), z_peer if x_first else x_peer)
        v.first, v.other = (v.x, v.z) if x_first else (v.z, v.x)
        v.d = [remote(quarter(dst, 0, *q), quarter(dst, 1, *q), *sem(5 + j), tensor_at(2))
               for j, q in enumerate(((0, 0), far, far[::-1], (1, 1)))]
        moves.append(v)
    for v in moves:
        v.a.start()
    weff_out = remote(z.weff, z.weffp, z.esem_s.at[0], z.esem_r.at[0], tensor_at(2))
    for v in moves:
        v.partner.start()
    weff_out.start()

    def relay1(i):
        moves[i].a.wait_recv()
        moves[i].first.start()
        moves[i].other.start()
        moves[i].d[0].start()

    def relay2(i):
        moves[i].first.wait_recv()
        moves[i].second.start()
        moves[i].d[1].start()

    def relay3(i):
        moves[i].other.wait_recv()
        moves[i].d[2].start()

    def relay4(i):
        moves[i].second.wait_recv()
        moves[i].d[3].start()

    def arrive(i):
        for c in moves[i].d:
            c.wait_recv()

    starts, ends = [], []
    total = jnp.int32(0)
    for s in range(slots):
        starts.append(total)
        total = total + z.lens[0, s]
        ends.append(total)
    n_valid = ends[slots - 2]
    lane = iota((1, LANES), 1)
    seg_start = jnp.zeros((1, LANES), jnp.int32)
    seg_end = jnp.zeros((1, LANES), jnp.int32)
    for s in range(slots):
        seg_start = jnp.where(lane == hd + s, starts[s], seg_start)
        seg_end = jnp.where(lane == hd + s, ends[s], seg_end)
    is_mask = (lane >= hd) & (lane < hd + slots)
    extra = jnp.where((lane >= hd + slots) & (lane < hd + slots + 3), 1.0, 0.0)
    ones_v = jnp.where((lane >= hd) & (lane < hd + 3), 1.0, 0.0)
    lanes = iota((BLK, LANES), 1)
    left = lanes < hd

    def span_of(b):
        return pl.ds(pl.multiple_of(b * BLK, BLK), BLK)

    def project(i, _):
        for j in range(4):
            @pl.when(i == j * (blocks // 4))
            def _():
                tok_in[j].wait()
        span = span_of(i)
        y = dot_nt(z.tok[span, :], z.weff[...])
        pos = i * BLK + iota((BLK, LANES), 0)
        mine = (pos >= seg_start) & (pos < seg_end)
        q_mask = jnp.where(mine, 1.0, 0.0)
        k_mask = jnp.where(is_mask & jnp.logical_not(mine), BLOCKED, extra)
        for c in range(pack // LANES):
            z.yt[c * LANES:(c + 1) * LANES, span] = y[:, c * LANES:(c + 1) * LANES].T.astype(bf16)

        def head(n):
            tile = y[:, (n // 2) * LANES:(n // 2 + 1) * LANES]
            return tile if n % 2 == 0 else pltpu.roll(tile, hd, 1)

        for h in range(heads):
            z.qa[h, span, :] = jnp.where(left, head(h) * hd ** -0.5, q_mask).astype(bf16)
            z.ka[h, span, :] = jnp.where(left, head(heads + h), k_mask).astype(bf16)
            z.va[h, span, :] = jnp.where(left, head(2 * heads + h), ones_v).astype(bf16)
            n = (2 * heads + h) * hd
            z.vt[h, 0:hd, span] = z.yt[n:n + hd, span]
        return 0

    lax.fori_loop(0, blocks, project, 0)
    relay1(0)

    def block_of(g, h):
        return per * g + h + lax.div(g, 2) * (1 - 2 * h)

    def key_range(qb):
        return jnp.maximum(qb - REACH, 0), jnp.minimum(qb + REACH + 1, blocks)

    def ctx_copy(k, h):
        return remote(z.xsend.at[k, h], z.xb.at[k, h], z.csem_s.at[k, h], z.csem_r.at[k, h], tensor_at(k))

    sub = iota((hd, BLK), 0)
    depth = z.vt.shape[1]

    def attend(n, _):
        h2, k2 = lax.div(n, 4), lax.rem(n, 4)
        fy = 1 - lax.div(k2, 2)
        fc = lax.rem(lax.rem(k2, 2) + lax.div(k2, 2), 2)
        g = 2 * lax.rem(yy + fy, 2) + lax.rem(cc + fc, 2)
        qb = block_of(g, h2)
        span = span_of(qb)
        lo, hi = key_range(qb)
        z.oacc[...] = jnp.zeros_like(z.oacc)
        z.peak[...] = jnp.full(z.peak.shape, BLOCKED, f32)

        def score(h, kb):
            z.sbuf[h] = dot_nt(z.ka[h, span_of(kb), :], z.qa[h, span, :])

        for h in range(heads):
            score(h, lo)

        def keys(kb, _):
            later = jnp.minimum(kb + 1, hi - 1)
            for h in range(heads):
                s = z.sbuf[h]
                old = z.peak[h:h + 1, :]
                new = jnp.maximum(old, jnp.max(s, axis=0, keepdims=True))
                p = jnp.exp2((s - new) * LOG2E).astype(bf16)
                z.peak[h:h + 1, :] = new
                scale = jnp.exp2((old - new) * LOG2E)
                z.oacc[h] = z.oacc[h] * scale + dot(z.vt[h, :, span_of(kb)], p)
                score(h, later)
            return 0

        lax.fori_loop(lo, hi, keys, 0)
        outs = []
        for h in range(heads):
            weight = z.oacc[h, hd:hd + 1, :]
            o = z.oacc[h, 0:hd, :] * (1.0 / weight)
            z.ot[h * hd:(h + 1) * hd, span] = o.astype(bf16)
            parts = three_parts(-(z.peak[h:h + 1, :] + jnp.log(weight)))
            tail = jnp.zeros((hd, BLK), f32)
            for j, p in enumerate(parts):
                tail = jnp.where(sub == slots + j, p, tail)
            t = jnp.concatenate([o, tail], axis=0).T
            outs.append(t)
            in_tail = (lanes >= hd + slots) & (lanes < hd + slots + 3)
            z.qa[h, span, :] = jnp.where(in_tail, t, z.qa[h, span, :].astype(f32)).astype(bf16)
        z.xsend[k2, h2, 0:BLK, :] = jnp.where(left, outs[0], pltpu.roll(outs[1], hd, 1)).astype(bf16)
        z.xsend[k2, h2, BLK:, :] = jnp.where(left[0:HALF], outs[2][0:HALF], pltpu.roll(outs[2][HALF:], hd, 1)).astype(bf16)

        @pl.when(k2 < 3)
        def _():
            remote(z.xsend.at[k2, h2], z.xb.at[k2, h2], z.csem_s.at[k2, h2], z.csem_r.at[k2, h2], {"tensor": g}).start()

        @pl.when(n == 2)
        def _():
            relay2(0)

        @pl.when(n == 3)
        def _():
            relay1(1)

        @pl.when(n == 4)
        def _():
            relay3(0)
            relay4(0)

        return 0

    lax.fori_loop(0, 2 * 4, attend, 0)

    wflat = z.wout.reshape(4 * 2 * LANES, feat)
    g1 = z.g1[...]
    g2 = z.g2[...]
    CH = 64

    def my_rows(h):
        return (h + yy * (1 - 2 * h)) * BLK

    def front(h, _):
        hs = span_of(h)

        @pl.when(h == 0)
        def _():
            own_w[0].wait()
            moves[0].partner.wait_recv()
            arrive(0)

        for k in range(3):
            ctx_copy(k, h).wait_recv()
        for k in range(4):
            src = z.xsend if k == 3 else z.xb
            z.xin[:, 2 * k * LANES:(2 * k + 1) * LANES] = src[k, h, 0:BLK, :]
            b = src[k, h, BLK:, :]
            z.xin[0:HALF, (2 * k + 1) * LANES:(2 * k + 2) * LANES] = b
            z.xin[HALF:, (2 * k + 1) * LANES:(2 * k + 2) * LANES] = pltpu.roll(b.astype(f32), hd, 1).astype(bf16)
        z.acc[hs, :] = dot(z.xin[...], wflat[...])
        row0 = me * own + my_rows(h)

        def norm_one(i, _):
            sp = pl.ds(pl.multiple_of(h * BLK + i * CH, CH), CH)
            tp = pl.ds(pl.multiple_of(row0 + i * CH, CH), CH)
            u, inv = moments(z.tok[tp, :].astype(f32) + z.acc[sp, :])
            z.unit1[sp, :] = u
            z.inv1[sp, :] = jnp.broadcast_to(inv, (CH, LANES))
            z.normed[sp, :] = u * g1
            z.low[sp, :] = (u * g1).astype(bf16)
            return 0

        lax.fori_loop(0, BLK // CH, norm_one, 0)

        @pl.when(h == 0)
        def _():
            relay2(1)
            own_w[1].wait()
            own_w[2].wait()
            moves[1].partner.wait_recv()
            moves[2].partner.wait_recv()

        pre = dot(z.low[hs, :], z.wfi[3])
        for k in (3, 2):
            later = dot(z.low[hs, :], z.wfi[2]) if k == 3 else None
            cdf, e = phi_parts(pre)
            z.gel[k, hs, :] = (cdf + pre * e * 0.3989422804014327).astype(bf16)
            out = dot((pre * cdf).astype(bf16), z.wfo[k])
            z.acc[hs, :] = out if k == 3 else z.acc[hs, :] + out
            pre = later

        @pl.when(h == 0)
        def _():
            relay3(1)
            relay1(2)

        return 0

    lax.fori_loop(0, 2, front, 0)
    relay4(1)
    cot_in.wait()

    def grad_copy(k, h):
        return remote(z.gsend.at[k, h], z.grecv.at[me, h], z.gsem_s.at[k, h], z.gsem_r.at[k, h], tensor_at(k))

    def rear(h, _):
        hs = span_of(h)

        @pl.when(h == 0)
        def _():
            arrive(1)

        pre = dot(z.low[hs, :], z.wfi[0])
        for k in range(2):
            later = dot(z.low[hs, :], z.wfi[1]) if k == 0 else None
            cdf, e = phi_parts(pre)
            z.gel[k, hs, :] = (cdf + pre * e * 0.3989422804014327).astype(bf16)
            z.actv[k] = (pre * cdf).astype(bf16)
            pre = later

        @pl.when(h == 0)
        def _():
            relay2(2)
            relay3(2)
            relay4(2)
            arrive(2)

        z.acc[hs, :] += dot(z.actv[0], z.wfo[0]) + dot(z.actv[1], z.wfo[1])
        row0 = my_rows(h)

        def norm_two(i, _):
            sp = pl.ds(pl.multiple_of(h * BLK + i * CH, CH), CH)
            tp = pl.ds(pl.multiple_of(row0 + i * CH, CH), CH)
            u, inv = moments(z.normed[sp, :] + z.acc[sp, :])
            pos = me * own + row0 + i * CH + iota((CH, 1), 0)
            valid = jnp.where(pos < n_valid, 1.0, 0.0)
            z.act[tp, :] = (u * g2 * valid).astype(bf16)
            gm = pull(z.cot[tp, :].astype(f32) * valid * g2, u, inv)
            z.acc[sp, :] = gm
            z.low[sp, :] = gm.astype(bf16)
            return 0

        lax.fori_loop(0, BLK // CH, norm_two, 0)
        ga = dot_nt(z.low[hs, :], z.wfo[0])
        for k in range(4):
            later = dot_nt(z.low[hs, :], z.wfo[k + 1]) if k < 3 else None
            z.acc[hs, :] += dot_nt((ga * z.gel[k, hs, :].astype(f32)).astype(bf16), z.wfi[k])
            ga = later

        def norm_back(i, _):
            sp = pl.ds(pl.multiple_of(h * BLK + i * CH, CH), CH)
            gm = pull(z.acc[sp, :] * g1, z.unit1[sp, :], z.inv1[sp, 0:1])
            z.normed[sp, :] = gm
            z.low[sp, :] = gm.astype(bf16)
            return 0

        lax.fori_loop(0, BLK // CH, norm_back, 0)
        for k in range(4):
            g = dot_nt(z.low[hs, :], z.wout[k])
            pair = g[:, 0:LANES].astype(bf16)
            last = jnp.where(left[0:HALF], g[0:HALF, LANES:], pltpu.roll(g[HALF:, LANES:], hd, 1)).astype(bf16)
            if k < 3:
                z.gsend[k, h, 0:BLK, :] = pair
                z.gsend[k, h, BLK:, :] = last
                grad_copy(k, h).start()
            else:
                z.grecv[me, h, 0:BLK, :] = pair
                z.grecv[me, h, BLK:, :] = last
        return 0

    lax.fori_loop(0, 2, rear, 0)

    z.gt[...] = jnp.zeros_like(z.gt)
    z.adp[...] = jnp.zeros_like(z.adp)
    last_block = blocks - 1
    role = lax.rem(cc + yy, 2)

    def place(o):
        og = lax.div(o, 2)
        odd = lax.rem(o, 2)
        return (o + (last_block - 2 * o) * (1 - yy), og + (3 - 2 * og) * (1 - yy), odd + lax.div(o, 4) * (1 - 2 * odd))

    def peer_grad(o):
        return remote(z.gown.at[o], z.gpeer.at[o], z.osem_s.at[o], z.osem_r.at[o], tensor_at(2))

    def part_copy(h):
        return remote(z.psend.at[h], z.precv.at[h], z.psem_s.at[h], z.psem_r.at[h], tensor_at(0))

    def finish(o):
        b, _, _ = place(o)
        span = span_of(b)
        scaled = 2 * width // LANES
        for c in range(pack // LANES):
            t = z.gt[c * LANES:(c + 1) * LANES, span].T
            z.gown[o, :, c * LANES:(c + 1) * LANES] = (t * hd ** -0.5 if c < scaled else t).astype(bf16)
        z.adp[...] += 2.0 * dot(z.yt[3 * width:3 * width + 2 * rank, span], z.gown[o])
        peer_grad(o).start()

    def contract(o):
        _, _, h = place(o)
        peer_grad(o).wait_recv()

        @pl.when(lax.rem(lax.div(o, 2) + role, 2) == 1)
        def _():
            both = dot(z.gown[o], z.weff[...]) + dot(z.gpeer[o], z.weffp[...])

            @pl.when(o < 4)
            def _():
                z.psend[h] = both.astype(bf16)
                part_copy(h).start()

            @pl.when(o >= 4)
            def _():
                hs = span_of(h)
                z.normed[hs, :] = z.normed[hs, :] + both

    def back(n, _):
        @pl.when(n == 0)
        def _():
            grad_copy(0, 0).wait_recv()
            grad_copy(1, 0).wait_recv()

        @pl.when(n == 2)
        def _():
            grad_copy(0, 1).wait_recv()
            grad_copy(1, 1).wait_recv()
            grad_copy(2, 0).wait_recv()
            grad_copy(2, 1).wait_recv()

        d, m4 = lax.div(n, 4), lax.rem(n, 4)
        mid = lax.rem(lax.div(m4 + 1, 2), 2)
        o = n + (1 - d) * mid * (3 - 2 * n)
        qb, g, h2 = place(o)
        span = span_of(qb)
        lo, hi = key_range(qb)
        pair_t = z.grecv[g, h2, 0:BLK, :].astype(f32).T
        last = z.grecv[g, h2, BLK:, :].astype(f32)
        last_t = jnp.concatenate([last, pltpu.roll(last, hd, 1)], axis=0).T[0:hd, :]
        for h in range(heads):
            do = last_t if h == 2 else pair_t[h * hd:(h + 1) * hd, :]
            z.dot_t[h * hd:(h + 1) * hd, :] = do.astype(bf16)
            delta = jnp.sum(do * z.ot[h * hd:(h + 1) * hd, span].astype(f32), axis=0, keepdims=True)
            tail = jnp.zeros((hd, BLK), f32)
            for j, p in enumerate(three_parts(-delta)):
                tail = jnp.where(sub == j, p, tail)
            z.doa[h] = jnp.concatenate([do, tail], axis=0).T.astype(bf16)

        def scores(h, kb):
            keys = span_of(kb)
            p = jnp.exp2(dot_nt(z.qa[h, span, :], z.ka[h, keys, :]) * LOG2E)
            z.pbuf[h] = p.astype(bf16)
            z.dsbuf[h] = (p * dot_nt(z.doa[h], z.va[h, keys, :])).astype(bf16)

        for h in range(heads):
            scores(h, lo)

        def step(kb, _):
            keys = span_of(kb)
            later = jnp.minimum(kb + 1, hi - 1)
            for h in range(heads):
                rq = slice(h * hd, (h + 1) * hd)
                rk = slice(width + h * hd, width + (h + 1) * hd)
                rv = slice(2 * width + h * hd, 2 * width + (h + 1) * hd)
                p, ds = z.pbuf[h], z.dsbuf[h]
                z.gt[rv, keys] += dot(z.dot_t[rq, :], p)
                z.gt[rk, keys] += dot(z.yt[rq, span], ds)
                z.gt[rq, span] += dot_nt(z.yt[rk, keys], ds)
                scores(h, later)
            return 0

        lax.fori_loop(lo, hi, step, 0)

        @pl.when(n >= 2)
        def _():
            finish(n - 2)

        @pl.when(n == 3)
        def _():
            weff_out.wait_recv()

        @pl.when(n >= 3)
        def _():
            contract(n - 3)

        return 0

    lax.fori_loop(0, blocks, back, 0)

    def finish_loop(o, _):
        finish(o)
        return 0

    lax.fori_loop(blocks - 2, blocks, finish_loop, 0)
    wide = 2 * LANES
    z.asend[:, 0:wide] = z.adp[0:rank, 0:wide]
    z.asend[:, wide:] = z.adp[rank:, pack - wide:]
    adapters = [remote(z.asend, z.arecv.at[d], z.asem_s.at[d], z.asem_r.at[d], row_at(d)) for d in range(1, n_dp)]
    for c in adapters:
        c.start()

    def contract_loop(o, _):
        contract(o)
        return 0

    lax.fori_loop(blocks - 3, blocks, contract_loop, 0)
    for h in range(2):
        part_copy(h).wait_recv()
        to = pl.ds(pl.multiple_of(my_rows(h), BLK), BLK)
        z.out[to, :] = z.normed[h * BLK:(h + 1) * BLK, :] + z.precv[h].astype(f32)
    total = z.asend[...]
    for c in adapters:
        c.wait_recv()
    for d in range(1, n_dp):
        total = total + z.arecv[d]
    cols = z.upq.shape[2]
    for base, ref in ((0, z.upq), (wide, z.upv)):
        for h in range(heads):
            at = base + h * hd
            tile = total[:, at // LANES * LANES:(at // LANES + 1) * LANES]
            ref[h] = pltpu.roll(tile, lax.rem(2 * LANES - at % LANES - dp * cols, LANES), 1)[:, 0:cols]

    for v in moves:
        for c in [v.a, v.partner, v.x, v.z, v.second] + v.d:
            c.wait_send()
    weff_out.wait_send()
    for h in range(2):
        for k in range(3):
            ctx_copy(k, h).wait_send()
            grad_copy(k, h).wait_send()
        part_copy(h).wait_send()
    for o in range(blocks):
        peer_grad(o).wait_send()
    for c in adapters:
        c.wait_send()


V = pl.BlockSpec(memory_space=pltpu.VMEM)
S = pl.BlockSpec(memory_space=pltpu.SMEM)
ANY = pl.BlockSpec(memory_space=pl.ANY)


def on_device(n_dp, groups, tokens, seq_lengths, query_weight, key_weight, value_weight, out_weight, ffn_in, ffn_out,
              gain_attn, gain_ffn, query_down, value_down, query_up, value_up, cotangent):
    rows, feat = tokens.shape
    width = query_weight.shape[1]
    rank, heads, hd = query_up.shape
    hidden = ffn_in.shape[1]
    own = rows // groups
    blocks = rows // BLK
    packed = (groups, own // BLK, BLK + HALF, LANES)
    pack = 5 * LANES
    cols = hd // n_dp
    dma = pltpu.SemaphoreType.DMA
    shape = jax.ShapeDtypeStruct
    inputs = [
        ("lens", seq_lengths, S), ("tok_hbm", tokens, ANY), ("cot_hbm", cotangent, ANY),
        ("wq", query_weight.T, V), ("wk", key_weight.T, V), ("wv", value_weight.T, V),
        ("dq", query_down.T, V), ("dv", value_down.T, V), ("uq", query_up.transpose(1, 0, 2), V), ("uv", value_up.transpose(1, 0, 2), V),
        ("ow", out_weight, ANY), ("fi", ffn_in, ANY), ("fo", ffn_out, ANY),
        ("g1", gain_attn.reshape(1, feat), V), ("g2", gain_ffn.reshape(1, feat), V),
    ]
    outputs = [
        ("act", shape((own, feat), bf16)), ("out", shape((own, feat), f32)),
        ("upq", shape((heads, rank, cols), f32)), ("upv", shape((heads, rank, cols), f32)),
    ]
    vm = pltpu.VMEM
    scratch = [
        ("tok", vm((rows, feat), bf16)), ("cot", vm((own, feat), bf16)),
        ("weff", vm((pack, feat), bf16)), ("weffp", vm((pack, feat), bf16)),
        ("qa", vm((heads, rows, LANES), bf16)), ("ka", vm((heads, rows, LANES), bf16)), ("va", vm((heads, rows, LANES), bf16)),
        ("yt", vm((pack, rows), bf16)), ("vt", vm((heads, hd + 16, rows), bf16)), ("ot", vm((width, rows), bf16)),
        ("sbuf", vm((heads, BLK, BLK), f32)), ("oacc", vm((heads, hd + 16, BLK), f32)), ("peak", vm((8, BLK), f32)),
        ("xin", vm((BLK, groups * 2 * LANES), bf16)), ("xsend", vm(packed, bf16)), ("xb", vm(packed, bf16)),
        ("wout", vm((groups, 2 * LANES, feat), bf16)), ("wfi", vm((groups, feat, hidden), bf16)), ("wfo", vm((groups, hidden, feat), bf16)),
        ("normed", vm((own, feat), f32)), ("unit1", vm((own, feat), f32)), ("inv1", vm((own, LANES), f32)),
        ("low", vm((own, feat), bf16)), ("acc", vm((own, feat), f32)), ("gel", vm((groups, own, hidden), bf16)),
        ("actv", vm((2, BLK, hidden), bf16)), ("gsend", vm(packed, bf16)), ("grecv", vm(packed, bf16)),
        ("doa", vm((heads, BLK, LANES), bf16)), ("dot_t", vm((width, BLK), bf16)),
        ("pbuf", vm((heads, BLK, BLK), bf16)), ("dsbuf", vm((heads, BLK, BLK), bf16)),
        ("gt", vm((pack, rows), f32)), ("adp", vm((2 * rank, pack), f32)),
        ("gown", vm((blocks, BLK, pack), bf16)), ("gpeer", vm((blocks, BLK, pack), bf16)),
        ("psend", vm((2, BLK, feat), bf16)), ("precv", vm((2, BLK, feat), bf16)),
        ("asend", vm((rank, 4 * LANES), f32)), ("arecv", vm((n_dp, rank, 4 * LANES), f32)),
        ("lsem", dma((8,))), ("wsem_s", dma((3, 9))), ("wsem_r", dma((3, 9))), ("esem_s", dma((1,))), ("esem_r", dma((1,))),
        ("csem_s", dma((3, 2))), ("csem_r", dma((3, 2))), ("gsem_s", dma((3, 2))), ("gsem_r", dma((3, 2))),
        ("osem_s", dma((blocks,))), ("osem_r", dma((blocks,))), ("psem_s", dma((2,))), ("psem_r", dma((2,))),
        ("asem_s", dma((n_dp,))), ("asem_r", dma((n_dp,))),
    ]
    names = [n for n, _, _ in inputs] + [n for n, _ in outputs] + [n for n, _ in scratch]
    act, grad_input, up_q, up_v = pl.pallas_call(
        functools.partial(layer_kernel, n_dp, heads, hd, names),
        out_shape=tuple(s for _, s in outputs),
        in_specs=[s for _, _, s in inputs],
        out_specs=(V,) * 4,
        scratch_shapes=[s for _, s in scratch],
        compiler_params=pltpu.CompilerParams(vmem_limit_bytes=VMEM_LIMIT, collective_id=0, has_side_effects=True),
        name="layer",
    )(*[a for _, a, _ in inputs])
    return act, grad_input, up_q.transpose(1, 0, 2), up_v.transpose(1, 0, 2)


def solution(mesh):
    in_specs = (
        P("dp", None), P("dp", None), P(None, "tensor"), P(None, "tensor"), P(None, "tensor"), P("tensor", None),
        P(None, "tensor"), P("tensor", None), P(), P(), P(), P(), P(None, "tensor", None), P(None, "tensor", None),
        P("dp", None),
    )
    out_specs = (P(("dp", "tensor"), None), P(("dp", "tensor"), None), P(None, "tensor", "dp"), P(None, "tensor", "dp"))
    return jax.shard_map(
        functools.partial(on_device, mesh.shape["dp"], mesh.shape["tensor"]),
        mesh=mesh, in_specs=in_specs, out_specs=out_specs, check_vma=False,
    )
```

time: 649 us -> 116 us (0.18); the launches traced: 639 us -> 115 us
  waiting for transfers between devices: 221 us -> 0 us
  matrix products: 173 us -> 0 us
  other arithmetic: 109 us -> 0 us
  Pallas kernels: 0 us -> 107 us
  local copies, waits for them, and re-layouts: 70.4 us -> 7.07 us
  blocking collectives: 37 us -> 0 us
  between operations: 15.5 us -> 0.65 us
  loops' own time: 12.2 us -> 0 us
    psum x4 -> x0, waiting for transfers between devices: 221 us -> none  [the longest x1 71 us: on_device(): lax.psum(jnp.dot(context, w_out, preferred_element_type=jnp.float32).asty...]
    dot_general x49 -> x0, matrix products: 173 us -> none  [the longest x8 34.9 us: block_scores(): jnp.einsum('qhd,khd->hqk', query_block, key_block, preferred_element_type...]
    pallas_call x0 -> x1, Pallas kernels: none -> 107 us  [on_device(): pl.pallas_call(functools.partial(layer_kernel, n_dp, heads, hd, names), o...]
    convert_element_type x7 -> x0, other arithmetic: 43.2 us -> none  [the longest x4 37.5 us: attend_backward(): grad_scores = (probability * (grad_prob - row_delta)).astype(jnp.bfloat16)]
    reduce_sum x11 -> x0, other arithmetic: 39.6 us -> none  [the longest x2 13 us: normalize_back(): jnp.mean(scaled, axis=-1, keepdims=True)]
    dynamic_slice x53 -> x0, local copies, waits for them, and re-layouts: 38.4 us -> none  [the longest x8 7.83 us: block_scores(): lax.dynamic_slice_in_dim(queries, row_start, block_span, 0)]
    unnamed x1 -> x0, blocking collectives: 37 us -> none
    another operation x2 -> x0, loops' own time: 12.2 us -> none  [the longest x1 9.72 us: on_device(): lax.scan(back_step, (empty_ext, empty_ext), jnp.arange(block_count))]
  transfers between devices with their start and end apart: 4 -> 0, of which waited for: 4 -> 0; matrix products, arithmetic and copies ran while one was open for 3% -> 0% of each run, Pallas kernels for 0% -> 0%
where the time goes in v2:
time: 116 us; the launch traced here: 115 us
  Pallas kernels  107 us (92%)
  local copies, waits for them, and re-layouts  7.07 us (6%)
    pallas_call x1, Pallas kernels, on_device(): pl.pallas_call(functools.partial(layer_kernel, n_dp, heads, hd, names), o...  107 us
    unnamed x10, local copies, waits for them, and re-layouts  4.53 us

profile of v2, /device:TPU:0, one launch (start us, length us, event | category | flops | bytes accessed | tf_op | source)
XLA Modules:
  0.0 114.6 jit_solution(13801199423868998623)
XLA Ops:
  0.6 1.3 %reshape.14.refs_13_ = f32[1,768]{1,0:T(1,128)} reshape(f32[768]{0:T(1024)} %param.23) | data formatting | bytes 6144 | tf_op jit(solution)/shard_map/reshape | solution.py:646
  1.9 1.3 %reshape.15.refs_14_ = f32[1,768]{1,0:T(1,128)} reshape(f32[768]{0:T(1024)} %param.24) | data formatting | bytes 6144 | tf_op jit(solution)/shard_map/reshape | solution.py:646
  3.2 106.9 %layer.1 = (bf16[512,768]{1,0:T(8,128)(2,1)}, f32[512,768]{1,0:T(8,128)}, f32[3,8,8]{2,1,0:T(8,128)}, f32[3,8,8]{2,1,0:T(8,128)}) custom-call(s32[1,9]{1,0:T(1,128)} %refs_0_.1, bf16[2048,768]{1,0:T(8,128)(2,1)} %refs_1_.1, bf16[2048,768]{1,0:T(8,128)(2,1)} %refs_2_.1, bf16[192,768]{1,0:T(8,128)(2,1)} %bitcast.9, bf16[192,768]{1,0:T(8,128)(2,1)} %bitcast.10, ...), custom_call_target="tpu_custom_call" | custom-call | tf_op jit(solution)/shard_map/layer/pallas_call | solution.py:676
  110.0 0.0 copy-start
  110.1 2.2 %copy.23 = bf16[512,768]{1,0:T(8,128)(2,1)} copy(bf16[512,768]{1,0:T(8,128)(2,1)} %get-tuple-element.16) | data formatting | bytes 1572864
  112.2 0.0 copy-done
  112.2 0.0 copy-start.2
  112.2 0.0 copy-start.1
  112.2 1.1 copy.24
  113.4 0.0 copy-done.2
  113.4 0.6 copy.25
  114.0 0.0 copy-done.1
  114.0 0.6 copy.26
Async XLA Ops:
  110.0 2.2 %copy-start = (f32[512,768]{1,0:T(8,128)S(1)}, f32[512,768]{1,0:T(8,128)}, u32[]{:S(2)}) copy-start(f32[512,768]{1,0:T(8,128)} %get-tuple-element.17) | copy-start | bytes 4718596
  112.2 1.1 %copy-start.2 = (f32[3,8,8]{2,1,0:T(8,128)S(1)}, f32[3,8,8]{2,1,0:T(8,128)}, u32[]{:S(2)}) copy-start(f32[3,8,8]{2,1,0:T(8,128)} %get-tuple-element.10) | copy-start | bytes 2308
  112.2 1.8 %copy-start.1 = (f32[3,8,8]{2,1,0:T(8,128)S(1)}, f32[3,8,8]{2,1,0:T(8,128)}, u32[]{:S(2)}) copy-start(f32[3,8,8]{2,1,0:T(8,128)} %get-tuple-element.11) | copy-start | bytes 2308

commit v3 on v2

--- a/solution.py
+++ b/solution.py
@@ -16,7 +16,7 @@
 REACH = 2
 f32 = jnp.float32
 bf16 = jnp.bfloat16
-VMEM_LIMIT = 64 * 1024 * 1024 - 65536
+VMEM_LIMIT = 59 * 1024 * 1024
 MESH = pl.DeviceIdType.MESH
 TN = (((0,), (0,)), ((), ()))
 
@@ -133,59 +133,68 @@
         z.wout[k, part:, :] = jnp.zeros((z.wout.shape[1] - part, feat), bf16)
     pl.semaphore_wait(barrier, 3 + n_dp - 1)
 
-    def quarter(dst, k, dx, dz):
-        n = (part if dst is z.wout else dst.shape[1]) // 4
+    def quarter(v, k, dx, dz, lo=0, n=None):
         q = 2 * lax.rem(pz + dz, 2) + lax.rem(px + dx, 2)
-        return dst.at[k, pl.ds(pl.multiple_of(q * n, n), n)]
-
-    def quarter_of(src):
-        n = src.shape[0] // 4
-        return src.at[pl.ds(pl.multiple_of((2 * pz + px) * n, n), n)]
-
+        return v.dst.at[k, pl.ds(pl.multiple_of(v.base + q * v.n + lo, 16), v.n if n is None else n)]
+
+    partners = [remote(src, full(dst, 2), z.bsem_s.at[i], z.bsem_r.at[i], tensor_at(2)) for i, (src, dst) in enumerate(weights)]
+    pieces = [(z.ow, z.wout, 0, part)]
+    for src, dst in weights[1:]:
+        rows2 = src.shape[0] // 2
+        pieces += [(src, dst, 0, rows2), (src, dst, rows2, rows2)]
     moves = []
-    for i, (src, dst) in enumerate(weights):
+    for i, (src, dst, base, rows2) in enumerate(pieces):
         v = Bag()
-        x_first = i < 2
+        v.dst, v.base, v.n = dst, base, rows2 // 4
+        cut = v.n // 32 * 16
         sem = lambda j, i=i: (z.wsem_s.at[i, j], z.wsem_r.at[i, j])
-        v.a = remote(quarter_of(src), quarter(dst, 0, 0, 0), *sem(0), tensor_at(0))
-        v.partner = remote(src, full(dst, 2), *sem(1), tensor_at(2))
-        v.x = remote(quarter(dst, 0, 0, 0), quarter(dst, 0, 0, 0), *sem(2), x_peer)
-        v.z = remote(quarter(dst, 0, 0, 0), quarter(dst, 0, 0, 0), *sem(3), z_peer)
-        far = (1, 0) if x_first else (0, 1)
-        v.second = remote(quarter(dst, 0, *far), quarter(dst, 0, *far), *sem(4), z_peer if x_first else x_peer)
-        v.first, v.other = (v.x, v.z) if x_first else (v.z, v.x)
-        v.d = [remote(quarter(dst, 0, *q), quarter(dst, 1, *q), *sem(5 + j), tensor_at(2))
-               for j, q in enumerate(((0, 0), far, far[::-1], (1, 1)))]
+        here = src.at[pl.ds(pl.multiple_of(base + (2 * pz + px) * v.n, 16), v.n)]
+        v.a = remote(here, quarter(v, 0, 0, 0), *sem(0), tensor_at(0))
+        v.x = remote(quarter(v, 0, 0, 0), quarter(v, 0, 0, 0), *sem(1), x_peer)
+        v.z = remote(quarter(v, 0, 0, 0), quarter(v, 0, 0, 0), *sem(2), z_peer)
+        v.far_x = remote(quarter(v, 0, 0, 1, 0, cut), quarter(v, 0, 0, 1, 0, cut), *sem(3), x_peer)
+        v.far_z = remote(quarter(v, 0, 1, 0, cut, v.n - cut), quarter(v, 0, 1, 0, cut, v.n - cut), *sem(4), z_peer)
+        v.d = [remote(quarter(v, 0, *q), quarter(v, 1, *q), *sem(5 + j), tensor_at(2))
+               for j, q in enumerate(((0, 0), (1, 0), (0, 1), (1, 1)))]
         moves.append(v)
     for v in moves:
         v.a.start()
     weff_out = remote(z.weff, z.weffp, z.esem_s.at[0], z.esem_r.at[0], tensor_at(2))
-    for v in moves:
-        v.partner.start()
+    for c in partners:
+        c.start()
     weff_out.start()
 
     def relay1(i):
-        moves[i].a.wait_recv()
-        moves[i].first.start()
-        moves[i].other.start()
-        moves[i].d[0].start()
+        v = moves[i]
+        v.a.wait_recv()
+        v.x.start()
+        v.z.start()
+        v.d[0].start()
 
     def relay2(i):
-        moves[i].first.wait_recv()
-        moves[i].second.start()
-        moves[i].d[1].start()
+        v = moves[i]
+        v.z.wait_recv()
+        v.far_x.start()
+        v.x.wait_recv()
+        v.far_z.start()
+        v.d[2].start()
+        v.d[1].start()
 
     def relay3(i):
-        moves[i].other.wait_recv()
-        moves[i].d[2].start()
-
-    def relay4(i):
-        moves[i].second.wait_recv()
-        moves[i].d[3].start()
+        v = moves[i]
+        v.far_x.wait_recv()
+        v.far_z.wait_recv()
+        v.d[3].start()
 
     def arrive(i):
         for c in moves[i].d:
             c.wait_recv()
+
+    def at(counter, value, *steps):
+        @pl.when(counter == value)
+        def _():
+            for step, i in steps:
+                step(i)
 
     starts, ends = [], []
     total = jnp.int32(0)
@@ -233,10 +242,11 @@
             z.va[h, span, :] = jnp.where(left, head(2 * heads + h), ones_v).astype(bf16)
             n = (2 * heads + h) * hd
             z.vt[h, 0:hd, span] = z.yt[n:n + hd, span]
+        at(i, blocks // 2, (relay1, 0))
+        at(i, blocks - 1, (relay1, 1))
         return 0
 
     lax.fori_loop(0, blocks, project, 0)
-    relay1(0)
 
     def block_of(g, h):
         return per * g + h + lax.div(g, 2) * (1 - 2 * h)
@@ -301,26 +311,21 @@
         def _():
             remote(z.xsend.at[k2, h2], z.xb.at[k2, h2], z.csem_s.at[k2, h2], z.csem_r.at[k2, h2], {"tensor": g}).start()
 
-        @pl.when(n == 2)
-        def _():
-            relay2(0)
-
-        @pl.when(n == 3)
-        def _():
-            relay1(1)
-
-        @pl.when(n == 4)
-        def _():
-            relay3(0)
-            relay4(0)
-
+        at(n, 0, (relay2, 0), (relay1, 2))
+        at(n, 1, (relay3, 0), (relay2, 1))
+        at(n, 2, (relay1, 3))
+        at(n, 3, (relay2, 2), (relay3, 1))
+        at(n, 4, (relay1, 4))
+        at(n, 5, (relay2, 3), (relay3, 2))
+        at(n, 6, (relay2, 4))
+        at(n, 7, (relay3, 3))
         return 0
 
     lax.fori_loop(0, 2 * 4, attend, 0)
 
     wflat = z.wout.reshape(4 * 2 * LANES, feat)
-    g1 = z.g1[...]
-    g2 = z.g2[...]
+    g1 = jnp.concatenate([z.g1[i:i + 1, :] for i in range(feat // LANES)], axis=1)
+    g2 = jnp.concatenate([z.g2[i:i + 1, :] for i in range(feat // LANES)], axis=1)
     CH = 64
 
     def my_rows(h):
@@ -332,7 +337,7 @@
         @pl.when(h == 0)
         def _():
             own_w[0].wait()
-            moves[0].partner.wait_recv()
+            partners[0].wait_recv()
             arrive(0)
 
         for k in range(3):
@@ -360,11 +365,11 @@
 
         @pl.when(h == 0)
         def _():
-            relay2(1)
+            relay3(4)
             own_w[1].wait()
             own_w[2].wait()
-            moves[1].partner.wait_recv()
-            moves[2].partner.wait_recv()
+            partners[1].wait_recv()
+            partners[2].wait_recv()
 
         pre = dot(z.low[hs, :], z.wfi[3])
         for k in (3, 2):
@@ -375,15 +380,9 @@
             z.acc[hs, :] = out if k == 3 else z.acc[hs, :] + out
             pre = later
 
-        @pl.when(h == 0)
-        def _():
-            relay3(1)
-            relay1(2)
-
         return 0
 
     lax.fori_loop(0, 2, front, 0)
-    relay4(1)
     cot_in.wait()
 
     def grad_copy(k, h):
@@ -395,6 +394,7 @@
         @pl.when(h == 0)
         def _():
             arrive(1)
+            arrive(2)
 
         pre = dot(z.low[hs, :], z.wfi[0])
         for k in range(2):
@@ -406,10 +406,8 @@
 
         @pl.when(h == 0)
         def _():
-            relay2(2)
-            relay3(2)
-            relay4(2)
-            arrive(2)
+            arrive(3)
+            arrive(4)
 
         z.acc[hs, :] += dot(z.actv[0], z.wfo[0]) + dot(z.actv[1], z.wfo[1])
         row0 = my_rows(h)
@@ -606,8 +604,10 @@
             ref[h] = pltpu.roll(tile, lax.rem(2 * LANES - at % LANES - dp * cols, LANES), 1)[:, 0:cols]
 
     for v in moves:
-        for c in [v.a, v.partner, v.x, v.z, v.second] + v.d:
+        for c in [v.a, v.x, v.z, v.far_x, v.far_z] + v.d:
             c.wait_send()
+    for c in partners:
+        c.wait_send()
     weff_out.wait_send()
     for h in range(2):
         for k in range(3):
@@ -618,6 +618,15 @@
         peer_grad(o).wait_send()
     for c in adapters:
         c.wait_send()
+
+
+def emit_kernel(act, out, upq, upv, act_hbm, out_hbm, upq_hbm, upv_hbm, sem):
+    copies = [pltpu.make_async_copy(src, dst, sem.at[i]) for i, (src, dst) in
+              enumerate(((out, out_hbm), (act, act_hbm), (upq, upq_hbm), (upv, upv_hbm)))]
+    for c in copies:
+        c.start()
+    for c in copies:
+        c.wait()
 
 
 V = pl.BlockSpec(memory_space=pltpu.VMEM)
@@ -643,7 +652,7 @@
         ("wq", query_weight.T, V), ("wk", key_weight.T, V), ("wv", value_weight.T, V),
         ("dq", query_down.T, V), ("dv", value_down.T, V), ("uq", query_up.transpose(1, 0, 2), V), ("uv", value_up.transpose(1, 0, 2), V),
         ("ow", out_weight, ANY), ("fi", ffn_in, ANY), ("fo", ffn_out, ANY),
-        ("g1", gain_attn.reshape(1, feat), V), ("g2", gain_ffn.reshape(1, feat), V),
+        ("g1", gain_attn.reshape(feat // LANES, LANES), V), ("g2", gain_ffn.reshape(feat // LANES, LANES), V),
     ]
     outputs = [
         ("act", shape((own, feat), bf16)), ("out", shape((own, feat), f32)),
@@ -667,21 +676,30 @@
         ("gown", vm((blocks, BLK, pack), bf16)), ("gpeer", vm((blocks, BLK, pack), bf16)),
         ("psend", vm((2, BLK, feat), bf16)), ("precv", vm((2, BLK, feat), bf16)),
         ("asend", vm((rank, 4 * LANES), f32)), ("arecv", vm((n_dp, rank, 4 * LANES), f32)),
-        ("lsem", dma((8,))), ("wsem_s", dma((3, 9))), ("wsem_r", dma((3, 9))), ("esem_s", dma((1,))), ("esem_r", dma((1,))),
+        ("lsem", dma((8,))), ("wsem_s", dma((5, 9))), ("wsem_r", dma((5, 9))), ("bsem_s", dma((3,))), ("bsem_r", dma((3,))), ("esem_s", dma((1,))), ("esem_r", dma((1,))),
         ("csem_s", dma((3, 2))), ("csem_r", dma((3, 2))), ("gsem_s", dma((3, 2))), ("gsem_r", dma((3, 2))),
         ("osem_s", dma((blocks,))), ("osem_r", dma((blocks,))), ("psem_s", dma((2,))), ("psem_r", dma((2,))),
         ("asem_s", dma((n_dp,))), ("asem_r", dma((n_dp,))),
     ]
     names = [n for n, _, _ in inputs] + [n for n, _ in outputs] + [n for n, _ in scratch]
-    act, grad_input, up_q, up_v = pl.pallas_call(
+    results = pl.pallas_call(
         functools.partial(layer_kernel, n_dp, heads, hd, names),
-        out_shape=tuple(s for _, s in outputs),
+        out_shape=tuple(vm(s.shape, s.dtype) for _, s in outputs),
         in_specs=[s for _, _, s in inputs],
         out_specs=(V,) * 4,
         scratch_shapes=[s for _, s in scratch],
         compiler_params=pltpu.CompilerParams(vmem_limit_bytes=VMEM_LIMIT, collective_id=0, has_side_effects=True),
         name="layer",
     )(*[a for _, a, _ in inputs])
+    act, grad_input, up_q, up_v = pl.pallas_call(
+        emit_kernel,
+        out_shape=tuple(s for _, s in outputs),
+        in_specs=[V] * 4,
+        out_specs=(ANY,) * 4,
+        scratch_shapes=[dma((4,))],
+        compiler_params=pltpu.CompilerParams(vmem_limit_bytes=4 * 1024 * 1024),
+        name="emit",
+    )(*results)
     return act, grad_input, up_q.transpose(1, 0, 2), up_v.transpose(1, 0, 2)
 
 

time: 116 us -> 99.4 us (0.86); the launches traced: 115 us -> 99.3 us
  Pallas kernels: 107 us -> 98.6 us
  local copies, waits for them, and re-layouts: 7.07 us -> 0 us
    pallas_call x1, Pallas kernels: 107 us -> 97.2 us  [on_device(): pl.pallas_call(functools.partial(layer_kernel, n_dp, heads, hd, names), o...]
    unnamed x10 -> x0, local copies, waits for them, and re-layouts: 4.53 us -> none
    reshape x2 -> x0, local copies, waits for them, and re-layouts: 2.53 us -> none  [the longest x1 1.27 us: on_device(): gain_attn.reshape(1, feat)]
    pallas_call x0 -> x1, Pallas kernels: none -> 1.44 us  [on_device(): pl.pallas_call(emit_kernel, out_shape=tuple((s for _, s in outputs)), in_...]
where the time goes in v3:
time: 99.4 us; the launch traced here: 99.3 us
  Pallas kernels  98.6 us (99%)
    pallas_call x1, Pallas kernels, on_device(): pl.pallas_call(functools.partial(layer_kernel, n_dp, heads, hd, names), o...  97.2 us

profile of v3, /device:TPU:0, one launch (start us, length us, event | category | flops | bytes accessed | tf_op | source)
XLA Modules:
  0.0 99.3 jit_solution(4102547963923245498)
XLA Ops:
  0.6 97.2 %layer.1 = (bf16[512,768]{1,0:T(8,128)(2,1)S(1)}, f32[512,768]{1,0:T(8,128)S(1)}, f32[3,8,8]{2,1,0:T(8,128)S(1)}, f32[3,8,8]{2,1,0:T(8,128)S(1)}) custom-call(s32[1,9]{1,0:T(1,128)} %refs_0_.1, bf16[2048,768]{1,0:T(8,128)(2,1)} %refs_1_.1, bf16[2048,768]{1,0:T(8,128)(2,1)} %refs_2_.1, bf16[192,768]{1,0:T(8,128)(2,1)} %bitcast.11, bf16[192,768]{1,0:T(8,128)(2,1)} %bitcast.12, ...), custom_call_target="tpu_custom_call" | custom-call | tf_op jit(solution)/shard_map/layer/pallas_call | solution.py:685
  97.8 1.4 %emit.1 = (bf16[512,768]{1,0:T(8,128)(2,1)}, f32[512,768]{1,0:T(8,128)}, f32[3,8,8]{2,1,0:T(8,128)}, f32[3,8,8]{2,1,0:T(8,128)}) custom-call(bf16[512,768]{1,0:T(8,128)(2,1)S(1)} %get-tuple-element.12.act, f32[512,768]{1,0:T(8,128)S(1)} %get-tuple-element.13.out, f32[3,8,8]{2,1,0:T(8,128)S(1)} %get-tuple-element.14.upq, f32[3,8,8]{2,1,0:T(8,128)S(1)} %get-tuple-element.15.upv), custom_call_target="tpu_custom_call" | custom-call | tf_op jit(solution)/shard_map/emit/pallas_call | solution.py:694

commit v4 on v3

--- a/solution.py
+++ b/solution.py
@@ -191,10 +191,12 @@
             c.wait_recv()
 
     def at(counter, value, *steps):
-        @pl.when(counter == value)
-        def _():
+        def once(_, carry):
             for step, i in steps:
                 step(i)
+            return carry
+
+        lax.fori_loop(0, jnp.where(counter == value, 1, 0), once, 0)
 
     starts, ends = [], []
     total = jnp.int32(0)
@@ -225,6 +227,7 @@
                 tok_in[j].wait()
         span = span_of(i)
         y = dot_nt(z.tok[span, :], z.weff[...])
+        z.gt[:, span] = jnp.zeros((pack, BLK), f32)
         pos = i * BLK + iota((BLK, LANES), 0)
         mine = (pos >= seg_start) & (pos < seg_end)
         q_mask = jnp.where(mine, 1.0, 0.0)
@@ -251,14 +254,15 @@
     def block_of(g, h):
         return per * g + h + lax.div(g, 2) * (1 - 2 * h)
 
-    def key_range(qb):
-        return jnp.maximum(qb - REACH, 0), jnp.minimum(qb + REACH + 1, blocks)
+    win = min(2 * REACH + 1, blocks)
+
+    def window(qb):
+        return jnp.minimum(jnp.maximum(qb - REACH, 0), blocks - win)
 
     def ctx_copy(k, h):
         return remote(z.xsend.at[k, h], z.xb.at[k, h], z.csem_s.at[k, h], z.csem_r.at[k, h], tensor_at(k))
 
     sub = iota((hd, BLK), 0)
-    depth = z.vt.shape[1]
 
     def attend(n, _):
         h2, k2 = lax.div(n, 4), lax.rem(n, 4)
@@ -267,36 +271,31 @@
         g = 2 * lax.rem(yy + fy, 2) + lax.rem(cc + fc, 2)
         qb = block_of(g, h2)
         span = span_of(qb)
-        lo, hi = key_range(qb)
-        z.oacc[...] = jnp.zeros_like(z.oacc)
-        z.peak[...] = jnp.full(z.peak.shape, BLOCKED, f32)
-
-        def score(h, kb):
-            z.sbuf[h] = dot_nt(z.ka[h, span_of(kb), :], z.qa[h, span, :])
-
-        for h in range(heads):
-            score(h, lo)
-
-        def keys(kb, _):
-            later = jnp.minimum(kb + 1, hi - 1)
-            for h in range(heads):
-                s = z.sbuf[h]
-                old = z.peak[h:h + 1, :]
-                new = jnp.maximum(old, jnp.max(s, axis=0, keepdims=True))
-                p = jnp.exp2((s - new) * LOG2E).astype(bf16)
-                z.peak[h:h + 1, :] = new
-                scale = jnp.exp2((old - new) * LOG2E)
-                z.oacc[h] = z.oacc[h] * scale + dot(z.vt[h, :, span_of(kb)], p)
-                score(h, later)
-            return 0
-
-        lax.fori_loop(lo, hi, keys, 0)
+        lo = window(qb)
+
+        def score(h):
+            top = None
+            for j in range(win):
+                s = dot_nt(z.ka[h, span_of(lo + j), :], z.qa[h, span, :])
+                z.sbuf[h, j] = s
+                best = jnp.max(s.reshape(BLK // 8, 8, BLK), axis=0)
+                top = best if top is None else jnp.maximum(top, best)
+            return jnp.max(top, axis=0, keepdims=True)
+
+        peaks = [score(0)]
         outs = []
         for h in range(heads):
-            weight = z.oacc[h, hd:hd + 1, :]
-            o = z.oacc[h, 0:hd, :] * (1.0 / weight)
+            if h + 1 < heads:
+                peaks.append(score(h + 1))
+            acc = None
+            for j in range(win):
+                p = jnp.exp2((z.sbuf[h, j] - peaks[h]) * LOG2E).astype(bf16)
+                o = dot(z.vt[h, :, span_of(lo + j)], p)
+                acc = o if acc is None else acc + o
+            weight = acc[hd:hd + 1, :]
+            o = acc[0:hd, :] * (1.0 / weight)
             z.ot[h * hd:(h + 1) * hd, span] = o.astype(bf16)
-            parts = three_parts(-(z.peak[h:h + 1, :] + jnp.log(weight)))
+            parts = three_parts(-(peaks[h] + jnp.log(weight)))
             tail = jnp.zeros((hd, BLK), f32)
             for j, p in enumerate(parts):
                 tail = jnp.where(sub == slots + j, p, tail)
@@ -311,14 +310,11 @@
         def _():
             remote(z.xsend.at[k2, h2], z.xb.at[k2, h2], z.csem_s.at[k2, h2], z.csem_r.at[k2, h2], {"tensor": g}).start()
 
-        at(n, 0, (relay2, 0), (relay1, 2))
-        at(n, 1, (relay3, 0), (relay2, 1))
-        at(n, 2, (relay1, 3))
-        at(n, 3, (relay2, 2), (relay3, 1))
-        at(n, 4, (relay1, 4))
-        at(n, 5, (relay2, 3), (relay3, 2))
-        at(n, 6, (relay2, 4))
-        at(n, 7, (relay3, 3))
+        at(n, 0, (relay2, 0))
+        at(n, 1, (relay1, 2))
+        at(n, 2, (relay2, 1))
+        at(n, 3, (relay1, 3))
+        at(n, 5, (relay1, 4), (relay2, 2))
         return 0
 
     lax.fori_loop(0, 2 * 4, attend, 0)
@@ -338,6 +334,7 @@
         def _():
             own_w[0].wait()
             partners[0].wait_recv()
+            relay3(0)
             arrive(0)
 
         for k in range(3):
@@ -365,12 +362,13 @@
 
         @pl.when(h == 0)
         def _():
-            relay3(4)
+            relay2(3)
             own_w[1].wait()
             own_w[2].wait()
             partners[1].wait_recv()
             partners[2].wait_recv()
 
+        at(h, 1, (relay3, 1), (relay2, 4), (relay3, 2))
         pre = dot(z.low[hs, :], z.wfi[3])
         for k in (3, 2):
             later = dot(z.low[hs, :], z.wfi[2]) if k == 3 else None
@@ -406,6 +404,8 @@
 
         @pl.when(h == 0)
         def _():
+            relay3(3)
+            relay3(4)
             arrive(3)
             arrive(4)
 
@@ -439,8 +439,11 @@
             return 0
 
         lax.fori_loop(0, BLK // CH, norm_back, 0)
+        later = dot_nt(z.low[hs, :], z.wout[0])
         for k in range(4):
-            g = dot_nt(z.low[hs, :], z.wout[k])
+            g = later
+            if k < 3:
+                later = dot_nt(z.low[hs, :], z.wout[k + 1])
             pair = g[:, 0:LANES].astype(bf16)
             last = jnp.where(left[0:HALF], g[0:HALF, LANES:], pltpu.roll(g[HALF:, LANES:], hd, 1)).astype(bf16)
             if k < 3:
@@ -454,7 +457,6 @@
 
     lax.fori_loop(0, 2, rear, 0)
 
-    z.gt[...] = jnp.zeros_like(z.gt)
     z.adp[...] = jnp.zeros_like(z.adp)
     last_block = blocks - 1
     role = lax.rem(cc + yy, 2)
@@ -516,7 +518,7 @@
         o = n + (1 - d) * mid * (3 - 2 * n)
         qb, g, h2 = place(o)
         span = span_of(qb)
-        lo, hi = key_range(qb)
+        lo = window(qb)
         pair_t = z.grecv[g, h2, 0:BLK, :].astype(f32).T
         last = z.grecv[g, h2, BLK:, :].astype(f32)
         last_t = jnp.concatenate([last, pltpu.roll(last, hd, 1)], axis=0).T[0:hd, :]
@@ -529,30 +531,27 @@
                 tail = jnp.where(sub == j, p, tail)
             z.doa[h] = jnp.concatenate([do, tail], axis=0).T.astype(bf16)
 
-        def scores(h, kb):
-            keys = span_of(kb)
+        def scores(h, j):
+            keys = span_of(lo + j)
             p = jnp.exp2(dot_nt(z.qa[h, span, :], z.ka[h, keys, :]) * LOG2E)
-            z.pbuf[h] = p.astype(bf16)
-            z.dsbuf[h] = (p * dot_nt(z.doa[h], z.va[h, keys, :])).astype(bf16)
+            z.pbuf[h, j] = p.astype(bf16)
+            z.dsbuf[h, :, j * BLK:(j + 1) * BLK] = (p * dot_nt(z.doa[h], z.va[h, keys, :])).astype(bf16)
 
         for h in range(heads):
-            scores(h, lo)
-
-        def step(kb, _):
-            keys = span_of(kb)
-            later = jnp.minimum(kb + 1, hi - 1)
+            scores(h, 0)
+        for j in range(win):
+            keys = span_of(lo + j)
             for h in range(heads):
                 rq = slice(h * hd, (h + 1) * hd)
                 rk = slice(width + h * hd, width + (h + 1) * hd)
                 rv = slice(2 * width + h * hd, 2 * width + (h + 1) * hd)
-                p, ds = z.pbuf[h], z.dsbuf[h]
-                z.gt[rv, keys] += dot(z.dot_t[rq, :], p)
-                z.gt[rk, keys] += dot(z.yt[rq, span], ds)
-                z.gt[rq, span] += dot_nt(z.yt[rk, keys], ds)
-                scores(h, later)
-            return 0
-
-        lax.fori_loop(lo, hi, step, 0)
+                if j + 1 < win:
+                    scores(h, j + 1)
+                z.gt[rv, keys] += dot(z.dot_t[rq, :], z.pbuf[h, j])
+                z.gt[rk, keys] += dot(z.yt[rq, span], z.dsbuf[h, :, j * BLK:(j + 1) * BLK])
+                if j + 1 == win:
+                    around = pl.ds(pl.multiple_of(lo * BLK, BLK), win * BLK)
+                    z.gt[rq, span] = dot_nt(z.yt[rk, around], z.dsbuf[h])
 
         @pl.when(n >= 2)
         def _():
@@ -587,6 +586,11 @@
         return 0
 
     lax.fori_loop(blocks - 3, blocks, contract_loop, 0)
+    for v in moves:
+        for c in [v.a, v.x, v.z, v.far_x, v.far_z] + v.d:
+            c.wait_send()
+    for c in partners:
+        c.wait_send()
     for h in range(2):
         part_copy(h).wait_recv()
         to = pl.ds(pl.multiple_of(my_rows(h), BLK), BLK)
@@ -603,11 +607,6 @@
             tile = total[:, at // LANES * LANES:(at // LANES + 1) * LANES]
             ref[h] = pltpu.roll(tile, lax.rem(2 * LANES - at % LANES - dp * cols, LANES), 1)[:, 0:cols]
 
-    for v in moves:
-        for c in [v.a, v.x, v.z, v.far_x, v.far_z] + v.d:
-            c.wait_send()
-    for c in partners:
-        c.wait_send()
     weff_out.wait_send()
     for h in range(2):
         for k in range(3):
@@ -645,6 +644,7 @@
     packed = (groups, own // BLK, BLK + HALF, LANES)
     pack = 5 * LANES
     cols = hd // n_dp
+    win = min(2 * REACH + 1, blocks)
     dma = pltpu.SemaphoreType.DMA
     shape = jax.ShapeDtypeStruct
     inputs = [
@@ -664,14 +664,14 @@
         ("weff", vm((pack, feat), bf16)), ("weffp", vm((pack, feat), bf16)),
         ("qa", vm((heads, rows, LANES), bf16)), ("ka", vm((heads, rows, LANES), bf16)), ("va", vm((heads, rows, LANES), bf16)),
         ("yt", vm((pack, rows), bf16)), ("vt", vm((heads, hd + 16, rows), bf16)), ("ot", vm((width, rows), bf16)),
-        ("sbuf", vm((heads, BLK, BLK), f32)), ("oacc", vm((heads, hd + 16, BLK), f32)), ("peak", vm((8, BLK), f32)),
+        ("sbuf", vm((heads, win, BLK, BLK), f32)),
         ("xin", vm((BLK, groups * 2 * LANES), bf16)), ("xsend", vm(packed, bf16)), ("xb", vm(packed, bf16)),
         ("wout", vm((groups, 2 * LANES, feat), bf16)), ("wfi", vm((groups, feat, hidden), bf16)), ("wfo", vm((groups, hidden, feat), bf16)),
         ("normed", vm((own, feat), f32)), ("unit1", vm((own, feat), f32)), ("inv1", vm((own, LANES), f32)),
         ("low", vm((own, feat), bf16)), ("acc", vm((own, feat), f32)), ("gel", vm((groups, own, hidden), bf16)),
         ("actv", vm((2, BLK, hidden), bf16)), ("gsend", vm(packed, bf16)), ("grecv", vm(packed, bf16)),
         ("doa", vm((heads, BLK, LANES), bf16)), ("dot_t", vm((width, BLK), bf16)),
-        ("pbuf", vm((heads, BLK, BLK), bf16)), ("dsbuf", vm((heads, BLK, BLK), bf16)),
+        ("pbuf", vm((heads, win, BLK, BLK), bf16)), ("dsbuf", vm((heads, BLK, win * BLK), bf16)),
         ("gt", vm((pack, rows), f32)), ("adp", vm((2 * rank, pack), f32)),
         ("gown", vm((blocks, BLK, pack), bf16)), ("gpeer", vm((blocks, BLK, pack), bf16)),
         ("psend", vm((2, BLK, feat), bf16)), ("precv", vm((2, BLK, feat), bf16)),

time: 99.4 us -> 90.7 us (0.912)
  Pallas kernels: 98.6 us -> 89.3 us
    pallas_call x1, Pallas kernels: 97.2 us -> 87.9 us  [on_device(): pl.pallas_call(functools.partial(layer_kernel, n_dp, heads, hd, names), o...]
where the time goes in v4:
time: 90.7 us; the launch traced here: 90.1 us
  Pallas kernels  89.3 us (98%)
    pallas_call x1, Pallas kernels, on_device(): pl.pallas_call(functools.partial(layer_kernel, n_dp, heads, hd, names), o...  87.9 us

profile of v4, /device:TPU:0, one launch (start us, length us, event | category | flops | bytes accessed | tf_op | source)
XLA Modules:
  0.0 90.1 jit_solution(13476497275629088821)
XLA Ops:
  0.6 87.9 %layer.1 = (bf16[512,768]{1,0:T(8,128)(2,1)S(1)}, f32[512,768]{1,0:T(8,128)S(1)}, f32[3,8,8]{2,1,0:T(8,128)S(1)}, f32[3,8,8]{2,1,0:T(8,128)S(1)}) custom-call(s32[1,9]{1,0:T(1,128)} %refs_0_.1, bf16[2048,768]{1,0:T(8,128)(2,1)} %refs_1_.1, bf16[2048,768]{1,0:T(8,128)(2,1)} %refs_2_.1, bf16[192,768]{1,0:T(8,128)(2,1)} %bitcast.11, bf16[192,768]{1,0:T(8,128)(2,1)} %bitcast.12, ...), custom_call_target="tpu_custom_call" | custom-call | tf_op jit(solution)/shard_map/layer/pallas_call | solution.py:685
  88.5 1.4 %emit.1 = (bf16[512,768]{1,0:T(8,128)(2,1)}, f32[512,768]{1,0:T(8,128)}, f32[3,8,8]{2,1,0:T(8,128)}, f32[3,8,8]{2,1,0:T(8,128)}) custom-call(bf16[512,768]{1,0:T(8,128)(2,1)S(1)} %get-tuple-element.12.act, f32[512,768]{1,0:T(8,128)S(1)} %get-tuple-element.13.out, f32[3,8,8]{2,1,0:T(8,128)S(1)} %get-tuple-element.14.upq, f32[3,8,8]{2,1,0:T(8,128)S(1)} %get-tuple-element.15.upv), custom_call_target="tpu_custom_call" | custom-call | tf_op jit(solution)/shard_map/emit/pallas_call | solution.py:694

commit v5 on v4

--- a/solution.py
+++ b/solution.py
@@ -75,7 +75,7 @@
     width = heads * hd
     slots = z.lens.shape[1]
     rank = z.dq.shape[0]
-    pack = z.weff.shape[0]
+    pack = z.weff.shape[0] // 2
     part = z.ow.shape[0]
     me = lax.axis_index("tensor")
     dp = lax.axis_index("dp")
@@ -126,7 +126,7 @@
             z.weff[base + h * hd:base + (h + 1) * hd, :] = mine.astype(bf16)
     downs = jnp.concatenate([z.dq[...].astype(f32), z.dv[...].astype(f32)], axis=0)
     z.weff[3 * width:3 * width + 2 * rank, :] = downs.astype(bf16)
-    z.weff[3 * width + 2 * rank:, :] = jnp.zeros((pack - 3 * width - 2 * rank, feat), bf16)
+    z.weff[3 * width + 2 * rank:pack, :] = jnp.zeros((pack - 3 * width - 2 * rank, feat), bf16)
     for h in range(heads):
         z.vt[h, hd:, :] = jnp.ones((z.vt.shape[1] - hd, rows), bf16)
     for k in range(4):
@@ -159,7 +159,7 @@
         moves.append(v)
     for v in moves:
         v.a.start()
-    weff_out = remote(z.weff, z.weffp, z.esem_s.at[0], z.esem_r.at[0], tensor_at(2))
+    weff_out = remote(z.weff.at[0:pack], z.weff.at[pack:2 * pack], z.esem_s.at[0], z.esem_r.at[0], tensor_at(2))
     for c in partners:
         c.start()
     weff_out.start()
@@ -226,7 +226,7 @@
             def _():
                 tok_in[j].wait()
         span = span_of(i)
-        y = dot_nt(z.tok[span, :], z.weff[...])
+        y = dot_nt(z.tok[span, :], z.weff[0:pack, :])
         z.gt[:, span] = jnp.zeros((pack, BLK), f32)
         pos = i * BLK + iota((BLK, LANES), 0)
         mine = (pos >= seg_start) & (pos < seg_end)
@@ -406,10 +406,15 @@
         def _():
             relay3(3)
             relay3(4)
+
+        z.acc[hs, :] += dot(z.actv[0], z.wfo[0])
+
+        @pl.when(h == 0)
+        def _():
             arrive(3)
             arrive(4)
 
-        z.acc[hs, :] += dot(z.actv[0], z.wfo[0]) + dot(z.actv[1], z.wfo[1])
+        z.acc[hs, :] += dot(z.actv[1], z.wfo[1])
         row0 = my_rows(h)
 
         def norm_two(i, _):
@@ -467,7 +472,7 @@
         return (o + (last_block - 2 * o) * (1 - yy), og + (3 - 2 * og) * (1 - yy), odd + lax.div(o, 4) * (1 - 2 * odd))
 
     def peer_grad(o):
-        return remote(z.gown.at[o], z.gpeer.at[o], z.osem_s.at[o], z.osem_r.at[o], tensor_at(2))
+        return remote(z.gboth.at[o, :, 0:pack], z.gboth.at[o, :, pack:2 * pack], z.osem_s.at[o], z.osem_r.at[o], tensor_at(2))
 
     def part_copy(h):
         return remote(z.psend.at[h], z.precv.at[h], z.psem_s.at[h], z.psem_r.at[h], tensor_at(0))
@@ -478,8 +483,8 @@
         scaled = 2 * width // LANES
         for c in range(pack // LANES):
             t = z.gt[c * LANES:(c + 1) * LANES, span].T
-            z.gown[o, :, c * LANES:(c + 1) * LANES] = (t * hd ** -0.5 if c < scaled else t).astype(bf16)
-        z.adp[...] += 2.0 * dot(z.yt[3 * width:3 * width + 2 * rank, span], z.gown[o])
+            z.gboth[o, :, c * LANES:(c + 1) * LANES] = (t * hd ** -0.5 if c < scaled else t).astype(bf16)
+        z.adp[...] += 2.0 * dot(z.yt[3 * width:3 * width + 2 * rank, span], z.gboth[o, :, 0:pack])
         peer_grad(o).start()
 
     def contract(o):
@@ -488,7 +493,7 @@
 
         @pl.when(lax.rem(lax.div(o, 2) + role, 2) == 1)
         def _():
-            both = dot(z.gown[o], z.weff[...]) + dot(z.gpeer[o], z.weffp[...])
+            both = dot(z.gboth[o], z.weff[...])
 
             @pl.when(o < 4)
             def _():
@@ -518,44 +523,57 @@
         o = n + (1 - d) * mid * (3 - 2 * n)
         qb, g, h2 = place(o)
         span = span_of(qb)
-        lo = window(qb)
-        pair_t = z.grecv[g, h2, 0:BLK, :].astype(f32).T
-        last = z.grecv[g, h2, BLK:, :].astype(f32)
-        last_t = jnp.concatenate([last, pltpu.roll(last, hd, 1)], axis=0).T[0:hd, :]
-        for h in range(heads):
-            do = last_t if h == 2 else pair_t[h * hd:(h + 1) * hd, :]
-            z.dot_t[h * hd:(h + 1) * hd, :] = do.astype(bf16)
-            delta = jnp.sum(do * z.ot[h * hd:(h + 1) * hd, span].astype(f32), axis=0, keepdims=True)
-            tail = jnp.zeros((hd, BLK), f32)
-            for j, p in enumerate(three_parts(-delta)):
-                tail = jnp.where(sub == j, p, tail)
-            z.doa[h] = jnp.concatenate([do, tail], axis=0).T.astype(bf16)
-
-        def scores(h, j):
-            keys = span_of(lo + j)
-            p = jnp.exp2(dot_nt(z.qa[h, span, :], z.ka[h, keys, :]) * LOG2E)
-            z.pbuf[h, j] = p.astype(bf16)
-            z.dsbuf[h, :, j * BLK:(j + 1) * BLK] = (p * dot_nt(z.doa[h], z.va[h, keys, :])).astype(bf16)
-
-        for h in range(heads):
-            scores(h, 0)
-        for j in range(win):
-            keys = span_of(lo + j)
+
+        def over(lo, count):
+            pair_t = z.grecv[g, h2, 0:BLK, :].astype(f32).T
+            last = z.grecv[g, h2, BLK:, :].astype(f32)
+            last_t = jnp.concatenate([last, pltpu.roll(last, hd, 1)], axis=0).T[0:hd, :]
             for h in range(heads):
-                rq = slice(h * hd, (h + 1) * hd)
-                rk = slice(width + h * hd, width + (h + 1) * hd)
-                rv = slice(2 * width + h * hd, 2 * width + (h + 1) * hd)
-                if j + 1 < win:
-                    scores(h, j + 1)
-                z.gt[rv, keys] += dot(z.dot_t[rq, :], z.pbuf[h, j])
-                z.gt[rk, keys] += dot(z.yt[rq, span], z.dsbuf[h, :, j * BLK:(j + 1) * BLK])
-                if j + 1 == win:
-                    around = pl.ds(pl.multiple_of(lo * BLK, BLK), win * BLK)
-                    z.gt[rq, span] = dot_nt(z.yt[rk, around], z.dsbuf[h])
-
-        @pl.when(n >= 2)
-        def _():
-            finish(n - 2)
+                do = last_t if h == 2 else pair_t[h * hd:(h + 1) * hd, :]
+                z.dot_t[h * hd:(h + 1) * hd, :] = do.astype(bf16)
+                delta = jnp.sum(do * z.ot[h * hd:(h + 1) * hd, span].astype(f32), axis=0, keepdims=True)
+                tail = jnp.zeros((hd, BLK), f32)
+                for j, p in enumerate(three_parts(-delta)):
+                    tail = jnp.where(sub == j, p, tail)
+                z.doa[h] = jnp.concatenate([do, tail], axis=0).T.astype(bf16)
+
+            def scores(h, j):
+                keys = span_of(lo + j)
+                p = jnp.exp2(dot_nt(z.qa[h, span, :], z.ka[h, keys, :]) * LOG2E)
+                z.pbuf[h, j] = p.astype(bf16)
+                z.dsbuf[h, :, j * BLK:(j + 1) * BLK] = (p * dot_nt(z.doa[h], z.va[h, keys, :])).astype(bf16)
+
+            for h in range(heads):
+                scores(h, 0)
+            for j in range(count):
+                keys = span_of(lo + j)
+                for h in range(heads):
+                    rq = slice(h * hd, (h + 1) * hd)
+                    rk = slice(width + h * hd, width + (h + 1) * hd)
+                    rv = slice(2 * width + h * hd, 2 * width + (h + 1) * hd)
+                    if j + 1 < count:
+                        scores(h, j + 1)
+                    z.gt[rv, keys] += dot(z.dot_t[rq, :], z.pbuf[h, j])
+                    z.gt[rk, keys] += dot(z.yt[rq, span], z.dsbuf[h, :, j * BLK:(j + 1) * BLK])
+                    if j + 1 == count:
+                        around = pl.ds(pl.multiple_of(lo * BLK, BLK), count * BLK)
+                        z.gt[rq, span] = dot_nt(z.yt[rk, around], z.dsbuf[h, :, 0:count * BLK])
+
+            @pl.when(n >= 2)
+            def _():
+                finish(n - 2)
+
+        low_edge = qb < REACH
+        edge = low_edge | (qb >= blocks - REACH)
+        few = min(2 * REACH, blocks)
+
+        @pl.when(edge)
+        def _():
+            over(jnp.where(low_edge, 0, blocks - few), few)
+
+        @pl.when(jnp.logical_not(edge))
+        def _():
+            over(window(qb), win)
 
         @pl.when(n == 3)
         def _():
@@ -661,7 +679,7 @@
     vm = pltpu.VMEM
     scratch = [
         ("tok", vm((rows, feat), bf16)), ("cot", vm((own, feat), bf16)),
-        ("weff", vm((pack, feat), bf16)), ("weffp", vm((pack, feat), bf16)),
+        ("weff", vm((2 * pack, feat), bf16)),
         ("qa", vm((heads, rows, LANES), bf16)), ("ka", vm((heads, rows, LANES), bf16)), ("va", vm((heads, rows, LANES), bf16)),
         ("yt", vm((pack, rows), bf16)), ("vt", vm((heads, hd + 16, rows), bf16)), ("ot", vm((width, rows), bf16)),
         ("sbuf", vm((heads, win, BLK, BLK), f32)),
@@ -673,7 +691,7 @@
         ("doa", vm((heads, BLK, LANES), bf16)), ("dot_t", vm((width, BLK), bf16)),
         ("pbuf", vm((heads, win, BLK, BLK), bf16)), ("dsbuf", vm((heads, BLK, win * BLK), bf16)),
         ("gt", vm((pack, rows), f32)), ("adp", vm((2 * rank, pack), f32)),
-        ("gown", vm((blocks, BLK, pack), bf16)), ("gpeer", vm((blocks, BLK, pack), bf16)),
+        ("gboth", vm((blocks, BLK, 2 * pack), bf16)),
         ("psend", vm((2, BLK, feat), bf16)), ("precv", vm((2, BLK, feat), bf16)),
         ("asend", vm((rank, 4 * LANES), f32)), ("arecv", vm((n_dp, rank, 4 * LANES), f32)),
         ("lsem", dma((8,))), ("wsem_s", dma((5, 9))), ("wsem_r", dma((5, 9))), ("bsem_s", dma((3,))), ("bsem_r", dma((3,))), ("esem_s", dma((1,))), ("esem_r", dma((1,))),

time: 90.7 us -> 89 us (0.981)
  Pallas kernels: 89.3 us -> 86.8 us
    pallas_call x1, Pallas kernels: 87.9 us -> 85.3 us  [on_device(): pl.pallas_call(functools.partial(layer_kernel, n_dp, heads, hd, names), o...]
where the time goes in v5:
time: 89 us; the launch traced here: 87.6 us
  Pallas kernels  86.8 us (98%)
    pallas_call x1, Pallas kernels, on_device(): pl.pallas_call(functools.partial(layer_kernel, n_dp, heads, hd, names), o...  85.3 us

profile of v5, /device:TPU:0, one launch (start us, length us, event | category | flops | bytes accessed | tf_op | source)
XLA Modules:
  0.0 87.6 jit_solution(5422270833503455593)
XLA Ops:
  0.6 85.3 %layer.1 = (bf16[512,768]{1,0:T(8,128)(2,1)S(1)}, f32[512,768]{1,0:T(8,128)S(1)}, f32[3,8,8]{2,1,0:T(8,128)S(1)}, f32[3,8,8]{2,1,0:T(8,128)S(1)}) custom-call(s32[1,9]{1,0:T(1,128)} %refs_0_.1, bf16[2048,768]{1,0:T(8,128)(2,1)} %refs_1_.1, bf16[2048,768]{1,0:T(8,128)(2,1)} %refs_2_.1, bf16[192,768]{1,0:T(8,128)(2,1)} %bitcast.11, bf16[192,768]{1,0:T(8,128)(2,1)} %bitcast.12, ...), custom_call_target="tpu_custom_call" | custom-call | tf_op jit(solution)/shard_map/layer/pallas_call | solution.py:703
  86.0 1.4 %emit.1 = (bf16[512,768]{1,0:T(8,128)(2,1)}, f32[512,768]{1,0:T(8,128)}, f32[3,8,8]{2,1,0:T(8,128)}, f32[3,8,8]{2,1,0:T(8,128)}) custom-call(bf16[512,768]{1,0:T(8,128)(2,1)S(1)} %get-tuple-element.12.act, f32[512,768]{1,0:T(8,128)S(1)} %get-tuple-element.13.out, f32[3,8,8]{2,1,0:T(8,128)S(1)} %get-tuple-element.14.upq, f32[3,8,8]{2,1,0:T(8,128)S(1)} %get-tuple-element.15.upv), custom_call_target="tpu_custom_call" | custom-call | tf_op jit(solution)/shard_map/emit/pallas_call | solution.py:712
